TPU v7x, 512 devices: a whole 4x8x8 slice. The times are simulated.
512 devices in a mesh: gx: 32 (over y, x), gy: 16 (over z, core).
Axes of the slice: x: 4, y: 8, z: 8, core: 2. Of those that a mesh axis runs over, the one named last changes fastest.
Arguments:
- source: float32 [256, 256, 256], P('gx', 'gy'), may hold values from -6 to 6
- initial: float32 [256, 256, 256], P('gx', 'gy'), may hold values from -6 to 6
- absorption: float32 [256, 256, 256], P('gx', 'gy'), may hold values from 0.01 to 0.2
- beta_x: float32 [256, 256, 256], P('gx', 'gy'), may hold values from 0.4 to 2.5
- beta_y: float32 [256, 256, 256], P('gx', 'gy'), may hold values from 0.4 to 2.5
- beta_z: float32 [256, 256, 256], P('gx', 'gy'), may hold values from 0.4 to 2.5
Outputs:
- solution: float32 [256, 256, 256], P('gx', 'gy')
All inputs are finite; a program needn't handle non-finite values.
Results may differ from a plain program's by a relative error of at most 0.00002.
Values sent between devices are 32-bit elements; how exact they have to be, the bound alone decides.
A program may use at most 64 MiB of HBM per device.

v0:
```python
import jax
import jax.numpy as jnp
from jax import lax
from jax.sharding import PartitionSpec as P

SWEEPS = 4
COARSE_SWEEPS = 8


def extended(block, sides, width):
    for axis, dim in sides:
        count = lax.axis_size(axis)
        forward = [(i, i + 1) for i in range(count - 1)]
        forward.append((count - 1, 0))
        backward = [(target, source) for source, target in forward]
        low = lax.ppermute(
            lax.slice_in_dim(block, block.shape[dim] - width, None, axis=dim), axis, forward
        )
        high = lax.ppermute(lax.slice_in_dim(block, 0, width, axis=dim), axis, backward)
        block = jnp.concatenate([low, block, high], axis=dim)
    return block


def passed_along(block, axis, distance):
    devices = range(lax.axis_size(axis))
    route = [((i - distance) % len(devices), i) for i in devices]
    return lax.ppermute(block, axis, route)


def restrict_cells(field):
    size_x, size_y, size_z = field.shape
    return field.reshape(size_x // 2, 2, size_y // 2, 2, size_z // 2, 2).mean(axis=(1, 3, 5))


def restrict_faces(face_x, face_y, face_z):
    lower_x = face_x[0::2]
    size_x, size_y, size_z = lower_x.shape
    coarse_x = lower_x.reshape(size_x, size_y // 2, 2, size_z // 2, 2).mean(axis=(2, 4))
    lower_y = face_y[:, 0::2]
    size_x, size_y, size_z = lower_y.shape
    coarse_y = lower_y.reshape(size_x // 2, 2, size_y, size_z // 2, 2).mean(axis=(1, 4))
    lower_z = face_z[:, :, 0::2]
    size_x, size_y, size_z = lower_z.shape
    coarse_z = lower_z.reshape(size_x // 2, 2, size_y // 2, 2, size_z).mean(axis=(1, 3))
    return (coarse_x, coarse_y, coarse_z)


def restrict_plane_x(plane):
    size_x, size_y, size_z = plane.shape
    return plane.reshape(1, size_y // 2, 2, size_z // 2, 2).mean(axis=(2, 4))


def restrict_plane_y(plane):
    size_x, size_y, size_z = plane.shape
    return plane.reshape(size_x // 2, 2, 1, size_z // 2, 2).mean(axis=(1, 4))


def prolong_cells(field):
    size_x, size_y, size_z = field.shape
    spread = jnp.broadcast_to(field[:, None, :, None, :, None], (size_x, 2, size_y, 2, size_z, 2))
    return spread.reshape(2 * size_x, 2 * size_y, 2 * size_z)


def level_coeffs(absorb, face_xl, face_yl, face_zl, next_x, next_y, stencil_scale):
    face_xh = jnp.concatenate([face_xl[1:], next_x], axis=0)
    face_yh = jnp.concatenate([face_yl[:, 1:], next_y], axis=1)
    face_zh = jnp.concatenate([face_zl[:, :, 1:], jnp.zeros_like(face_zl[:, :, :1])], axis=2)
    diagonal = absorb + stencil_scale * (face_xl + face_xh + face_yl + face_yh + face_zl + face_zh)
    return (absorb, face_xl, face_xh, face_yl, face_yh, face_zl, face_zh, diagonal, stencil_scale)


def split_padded(padded):
    return (padded[:-2, 1:-1], padded[2:, 1:-1], padded[1:-1, :-2], padded[1:-1, 2:])


def neighbours(field, level):
    if level == 0:
        padded = extended(field, (("gx", 0), ("gy", 1)), 1)
    elif level == 1:
        padded = extended(field, (("gx", 0), ("gy", 1)), 1)
    else:
        padded = extended(field, (("gx", 0), ("gy", 1)), 1)
    return split_padded(padded)


def apply_operator(field, coeffs, lower_x, upper_x, lower_y, upper_y):
    absorb, face_xl, face_xh, face_yl, face_yh, face_zl, face_zh, diagonal, stencil_scale = coeffs
    zeros_plane = jnp.zeros_like(field[:, :, :1])
    lower_z = jnp.concatenate([zeros_plane, field[:, :, :-1]], axis=2)
    upper_z = jnp.concatenate([field[:, :, 1:], zeros_plane], axis=2)
    flux = (
        face_xl * (field - lower_x)
        + face_xh * (field - upper_x)
        + face_yl * (field - lower_y)
        + face_yh * (field - upper_y)
        + face_zl * (field - lower_z)
        + face_zh * (field - upper_z)
    )
    return absorb * field + stencil_scale * flux


def chebyshev_weights(sweeps):
    cheb_theta = 1.125
    cheb_delta = 0.875
    cheb_sigma = cheb_theta / cheb_delta
    rho_old = 1.0 / cheb_sigma
    weights = [(0.0, 1.0 / cheb_theta)]
    for sweep in range(1, sweeps):
        rho_new = 1.0 / (2.0 * cheb_sigma - rho_old)
        weights.append((rho_new * rho_old, 2.0 * rho_new / cheb_delta))
        rho_old = rho_new
    return weights


def chebyshev_smooth(iterate, target, coeffs, sweeps, zero_start, finder):
    update = jnp.zeros_like(target)
    for sweep, pair in enumerate(chebyshev_weights(sweeps)):
        if sweep == 0 and zero_start:
            remain = target
        else:
            remain = target - apply_operator(iterate, coeffs, *finder(iterate))
        update = pair[0] * update + pair[1] * remain / coeffs[7]
        iterate = iterate + update
    return iterate


def local(source, initial, absorption, beta_x, beta_y, beta_z):
    next_x = passed_along(beta_x[0:1], "gx", -1)
    next_y = passed_along(beta_y[:, 0:1], "gy", -1)
    coeffs_fine = level_coeffs(absorption, beta_x, beta_y, beta_z, next_x, next_y, 1.0)
    absorb_mid = restrict_cells(absorption)
    face_mid = restrict_faces(beta_x, beta_y, beta_z)
    next_x_mid = restrict_plane_x(next_x)
    next_y_mid = restrict_plane_y(next_y)
    coeffs_mid = level_coeffs(
        absorb_mid, face_mid[0], face_mid[1], face_mid[2], next_x_mid, next_y_mid, 0.25
    )
    absorb_low = restrict_cells(absorb_mid)
    face_low = restrict_faces(face_mid[0], face_mid[1], face_mid[2])

    def fine_finder(field):
        return neighbours(field, 0)

    def mid_finder(field):
        return neighbours(field, 1)

    def low_finder(field):
        return neighbours(field, 2)

    fine_iter = chebyshev_smooth(initial, source, coeffs_fine, SWEEPS, False, fine_finder)
    fine_rest = source - apply_operator(fine_iter, coeffs_fine, *fine_finder(fine_iter))
    source_mid = restrict_cells(fine_rest)
    mid_iter = chebyshev_smooth(
        jnp.zeros_like(source_mid), source_mid, coeffs_mid, SWEEPS, True, mid_finder
    )
    mid_rest = source_mid - apply_operator(mid_iter, coeffs_mid, *mid_finder(mid_iter))
    source_low = restrict_cells(mid_rest)
    next_x_low = restrict_plane_x(next_x_mid)
    next_y_low = restrict_plane_y(next_y_mid)
    coeffs_low = level_coeffs(
        absorb_low, face_low[0], face_low[1], face_low[2], next_x_low, next_y_low, 0.0625
    )
    low_iter = chebyshev_smooth(
        jnp.zeros_like(source_low), source_low, coeffs_low, COARSE_SWEEPS, True, low_finder
    )
    mid_iter = mid_iter + prolong_cells(low_iter)
    mid_iter = chebyshev_smooth(mid_iter, source_mid, coeffs_mid, SWEEPS, False, mid_finder)
    fine_iter = fine_iter + prolong_cells(mid_iter)
    return chebyshev_smooth(fine_iter, source, coeffs_fine, SWEEPS, False, fine_finder)


def solution(mesh):
    return jax.shard_map(
        local,
        mesh=mesh,
        in_specs=(
            P("gx", "gy", None),
            P("gx", "gy", None),
            P("gx", "gy", None),
            P("gx", "gy", None),
            P("gx", "gy", None),
            P("gx", "gy", None),
        ),
        out_specs=P("gx", "gy", None),
        check_vma=False,
    )
```

profile of v0, /device:TPU:1, one launch (start us, length us, event | category | flops | bytes accessed | tf_op | source)
XLA Modules:
  0.0 432.5 jit_solution(6670439468296285537)
XLA Ops:
  1.4 8.1 %collective-permute-start.1 = (f32[1,16,256]{2,1,0:T(8,128)}, f32[1,16,256]{2,1,0:T(8,128)S(1)}, u32[]{:S(2)}, u32[]{:S(2)}) collective-permute-start(f32[1,16,256]{2,1,0:T(8,128)} %slice.870), channel_id=1, source_target_pairs={{16,0},{32,16},{48,32},{64,48},{80,64},{96,80},{112,96},{128,112},... | collective-permute-start | bytes 49160 | tf_op jit(solution)/shard_map/ppermute | solution.py:27
  12.1 3.3 collective-permute-start
  15.4 5.3 %collective-permute-start.2 = (f32[1,16,256]{2,1,0:T(8,128)S(1)}, f32[1,16,256]{2,1,0:T(8,128)S(1)}, u32[]{:S(2)}, u32[]{:S(2)}) collective-permute-start(f32[1,16,256]{2,1,0:T(8,128)S(1)} %get-tuple-element.91), channel_id=1, source_target_pairs={{16,0},{32,16},{48,32},{64,48},{80,64},{96,80},{112,96},{128,112},... | collective-permute-start | bytes 49160 | tf_op jit(solution)/shard_map/ppermute | solution.py:19
  23.3 2.8 reduce_sum.128
  29.6 2.6 collective-permute-start.3
  32.2 6.2 %collective-permute-start.5 = (f32[10,1,256]{2,1,0:T(1,128)S(1)}, f32[10,1,256]{2,1,0:T(1,128)S(1)}, u32[]{:S(2)}, u32[]{:S(2)}) collective-permute-start(f32[10,1,256]{2,1,0:T(1,128)S(1)} %get-tuple-element.58), channel_id=1, source_target_pairs={{1,0},{2,1},{3,2},{4,3},{5,4},{6,5},{7,6},{8,7},{9,8},{10,9},{11,1... | collective-permute-start | bytes 30728 | tf_op jit(solution)/shard_map/ppermute | solution.py:19
  38.6 2.2 slice.926
  41.9 1.9 collective-permute-start.6
  43.9 6.7 %collective-permute-start.7 = (f32[1,16,256]{2,1,0:T(8,128)S(1)}, f32[1,16,256]{2,1,0:T(8,128)S(1)}, u32[]{:S(2)}, u32[]{:S(2)}) collective-permute-start(f32[1,16,256]{2,1,0:T(8,128)S(1)} %get-tuple-element.88), channel_id=1, source_target_pairs={{16,0},{32,16},{48,32},{64,48},{80,64},{96,80},{112,96},{128,112},... | collective-permute-start | bytes 49160 | tf_op jit(solution)/shard_map/ppermute | solution.py:19
  51.4 4.1 collective-permute-start.9
  56.6 1.9 collective-permute-start.10
  58.5 7.2 %collective-permute-start.11 = (f32[1,16,256]{2,1,0:T(8,128)S(1)}, f32[1,16,256]{2,1,0:T(8,128)S(1)}, u32[]{:S(2)}, u32[]{:S(2)}) collective-permute-start(f32[1,16,256]{2,1,0:T(8,128)S(1)} %get-tuple-element.84), channel_id=1, source_target_pairs={{16,0},{32,16},{48,32},{64,48},{80,64},{96,80},{112,96},{128,112},... | collective-permute-start | bytes 49160 | tf_op jit(solution)/shard_map/ppermute | solution.py:19
  65.8 9.8 %reshape.120 = f32[4,2,8,2,128,2]{5,4,3,2,1,0:T(8,128)} reshape(f32[8,16,256]{2,1,0:T(8,128)S(1)} %copy-done.3) | data formatting | bytes 262144 | tf_op jit(solution)/shard_map/reshape | solution.py:32
  75.7 4.1 reduce_sum.127
  80.9 3.8 collective-permute-start.13
  87.7 6.7 %collective-permute-start.15 = (f32[1,16,256]{2,1,0:T(8,128)S(1)}, f32[1,16,256]{2,1,0:T(8,128)S(1)}, u32[]{:S(2)}, u32[]{:S(2)}) collective-permute-start(f32[1,16,256]{2,1,0:T(8,128)S(1)} %get-tuple-element.82), channel_id=1, source_target_pairs={{16,0},{32,16},{48,32},{64,48},{80,64},{96,80},{112,96},{128,112},... | collective-permute-start | bytes 49160 | tf_op jit(solution)/shard_map/ppermute | solution.py:19
  95.7 4.2 collective-permute-start.17
  102.9 7.4 %collective-permute-start.19 = (f32[1,16,256]{2,1,0:T(8,128)S(1)}, f32[1,16,256]{2,1,0:T(8,128)S(1)}, u32[]{:S(2)}, u32[]{:S(2)}) collective-permute-start(f32[1,16,256]{2,1,0:T(8,128)S(1)} %get-tuple-element.78), channel_id=1, source_target_pairs={{16,0},{32,16},{48,32},{64,48},{80,64},{96,80},{112,96},{128,112},... | collective-permute-start | bytes 49160 | tf_op jit(solution)/shard_map/ppermute | solution.py:19
  111.1 4.4 %collective-permute-start.21 = (f32[10,1,256]{2,1,0:T(1,128)S(1)}, f32[10,1,256]{2,1,0:T(1,128)S(1)}, u32[]{:S(2)}, u32[]{:S(2)}) collective-permute-start(f32[10,1,256]{2,1,0:T(1,128)S(1)} %get-tuple-element.50), channel_id=1, source_target_pairs={{1,0},{2,1},{3,2},{4,3},{5,4},{6,5},{7,6},{8,7},{9,8},{10,9},{11,1... | collective-permute-start | bytes 30728 | tf_op jit(solution)/shard_map/ppermute | solution.py:19
  116.4 9.8 %reshape.119 = f32[4,2,8,2,128,2]{5,4,3,2,1,0:T(8,128)} reshape(f32[8,16,256]{2,1,0:T(8,128)S(1)} %fusion.78) | data formatting | bytes 262144 | tf_op jit(solution)/shard_map/reshape | solution.py:32
  126.2 4.1 reduce_sum.126
  132.2 7.2 %collective-permute-start.23 = (f32[1,8,128]{2,1,0:T(8,128)S(1)}, f32[1,8,128]{2,1,0:T(8,128)S(1)}, u32[]{:S(2)}, u32[]{:S(2)}) collective-permute-start(f32[1,8,128]{2,1,0:T(8,128)S(1)} %get-tuple-element.142), channel_id=1, source_target_pairs={{16,0},{32,16},{48,32},{64,48},{80,64},{96,80},{112,96},{128,112},... | collective-permute-start | bytes 12296 | tf_op jit(solution)/shard_map/ppermute | solution.py:19
  140.2 4.4 %collective-permute-start.25 = (f32[6,1,128]{2,1,0:T(1,128)S(1)}, f32[6,1,128]{2,1,0:T(1,128)S(1)}, u32[]{:S(2)}, u32[]{:S(2)}) collective-permute-start(f32[6,1,128]{2,1,0:T(1,128)S(1)} %get-tuple-element.110), channel_id=1, source_target_pairs={{1,0},{2,1},{3,2},{4,3},{5,4},{6,5},{7,6},{8,7},{9,8},{10,9},{11,1... | collective-permute-start | bytes 9224 | tf_op jit(solution)/shard_map/ppermute | solution.py:19
  147.4 7.2 %collective-permute-start.27 = (f32[1,8,128]{2,1,0:T(8,128)S(1)}, f32[1,8,128]{2,1,0:T(8,128)S(1)}, u32[]{:S(2)}, u32[]{:S(2)}) collective-permute-start(f32[1,8,128]{2,1,0:T(8,128)S(1)} %get-tuple-element.138), channel_id=1, source_target_pairs={{16,0},{32,16},{48,32},{64,48},{80,64},{96,80},{112,96},{128,112},... | collective-permute-start | bytes 12296 | tf_op jit(solution)/shard_map/ppermute | solution.py:19
  155.4 4.3 collective-permute-start.29
  162.6 7.2 %collective-permute-start.31 = (f32[1,8,128]{2,1,0:T(8,128)S(1)}, f32[1,8,128]{2,1,0:T(8,128)S(1)}, u32[]{:S(2)}, u32[]{:S(2)}) collective-permute-start(f32[1,8,128]{2,1,0:T(8,128)S(1)} %get-tuple-element.136), channel_id=1, source_target_pairs={{16,0},{32,16},{48,32},{64,48},{80,64},{96,80},{112,96},{128,112},... | collective-permute-start | bytes 12296 | tf_op jit(solution)/shard_map/ppermute | solution.py:19
  170.6 4.3 collective-permute-start.33
  177.7 7.2 %collective-permute-start.35 = (f32[1,8,128]{2,1,0:T(8,128)S(1)}, f32[1,8,128]{2,1,0:T(8,128)S(1)}, u32[]{:S(2)}, u32[]{:S(2)}) collective-permute-start(f32[1,8,128]{2,1,0:T(8,128)S(1)} %get-tuple-element.132), channel_id=1, source_target_pairs={{16,0},{32,16},{48,32},{64,48},{80,64},{96,80},{112,96},{128,112},... | collective-permute-start | bytes 12296 | tf_op jit(solution)/shard_map/ppermute | solution.py:19
  186.2 3.8 collective-permute-start.37
  192.1 1.9 collective-permute-start.38
  194.0 7.2 %collective-permute-start.39 = (f32[1,4,64]{2,1,0:T(4,128)S(1)}, f32[1,4,64]{2,1,0:T(4,128)S(1)}, u32[]{:S(2)}, u32[]{:S(2)}) collective-permute-start(f32[1,4,64]{2,1,0:T(4,128)S(1)} %get-tuple-element.184), channel_id=1, source_target_pairs={{16,0},{32,16},{48,32},{64,48},{80,64},{96,80},{112,96},{128,112},... | collective-permute-start | bytes 3080 | tf_op jit(solution)/shard_map/ppermute | solution.py:19
  202.0 4.3 collective-permute-start.41
  209.1 7.2 %collective-permute-start.43 = (f32[1,4,64]{2,1,0:T(4,128)S(1)}, f32[1,4,64]{2,1,0:T(4,128)S(1)}, u32[]{:S(2)}, u32[]{:S(2)}) collective-permute-start(f32[1,4,64]{2,1,0:T(4,128)S(1)} %get-tuple-element.180), channel_id=1, source_target_pairs={{16,0},{32,16},{48,32},{64,48},{80,64},{96,80},{112,96},{128,112},... | collective-permute-start | bytes 3080 | tf_op jit(solution)/shard_map/ppermute | solution.py:19
  217.1 4.3 collective-permute-start.45
  224.2 7.2 %collective-permute-start.47 = (f32[1,4,64]{2,1,0:T(4,128)S(1)}, f32[1,4,64]{2,1,0:T(4,128)S(1)}, u32[]{:S(2)}, u32[]{:S(2)}) collective-permute-start(f32[1,4,64]{2,1,0:T(4,128)S(1)} %get-tuple-element.176), channel_id=1, source_target_pairs={{16,0},{32,16},{48,32},{64,48},{80,64},{96,80},{112,96},{128,112},... | collective-permute-start | bytes 3080 | tf_op jit(solution)/shard_map/ppermute | solution.py:19
  232.2 4.3 collective-permute-start.49
  239.3 7.2 %collective-permute-start.51 = (f32[1,4,64]{2,1,0:T(4,128)S(1)}, f32[1,4,64]{2,1,0:T(4,128)S(1)}, u32[]{:S(2)}, u32[]{:S(2)}) collective-permute-start(f32[1,4,64]{2,1,0:T(4,128)S(1)} %get-tuple-element.172), channel_id=1, source_target_pairs={{16,0},{32,16},{48,32},{64,48},{80,64},{96,80},{112,96},{128,112},... | collective-permute-start | bytes 3080 | tf_op jit(solution)/shard_map/ppermute | solution.py:19
  247.3 4.3 collective-permute-start.53
  254.4 7.2 %collective-permute-start.55 = (f32[1,4,64]{2,1,0:T(4,128)S(1)}, f32[1,4,64]{2,1,0:T(4,128)S(1)}, u32[]{:S(2)}, u32[]{:S(2)}) collective-permute-start(f32[1,4,64]{2,1,0:T(4,128)S(1)} %get-tuple-element.168), channel_id=1, source_target_pairs={{16,0},{32,16},{48,32},{64,48},{80,64},{96,80},{112,96},{128,112},... | collective-permute-start | bytes 3080 | tf_op jit(solution)/shard_map/ppermute | solution.py:19
  262.4 4.3 collective-permute-start.57
  269.5 7.2 %collective-permute-start.59 = (f32[1,4,64]{2,1,0:T(4,128)S(1)}, f32[1,4,64]{2,1,0:T(4,128)S(1)}, u32[]{:S(2)}, u32[]{:S(2)}) collective-permute-start(f32[1,4,64]{2,1,0:T(4,128)S(1)} %get-tuple-element.164), channel_id=1, source_target_pairs={{16,0},{32,16},{48,32},{64,48},{80,64},{96,80},{112,96},{128,112},... | collective-permute-start | bytes 3080 | tf_op jit(solution)/shard_map/ppermute | solution.py:19
  277.5 4.3 collective-permute-start.61
  284.6 7.2 %collective-permute-start.63 = (f32[1,4,64]{2,1,0:T(4,128)S(1)}, f32[1,4,64]{2,1,0:T(4,128)S(1)}, u32[]{:S(2)}, u32[]{:S(2)}) collective-permute-start(f32[1,4,64]{2,1,0:T(4,128)S(1)} %get-tuple-element.162), channel_id=1, source_target_pairs={{16,0},{32,16},{48,32},{64,48},{80,64},{96,80},{112,96},{128,112},... | collective-permute-start | bytes 3080 | tf_op jit(solution)/shard_map/ppermute | solution.py:19
  292.6 4.3 collective-permute-start.65
  300.4 7.2 %collective-permute-start.67 = (f32[1,8,128]{2,1,0:T(8,128)S(1)}, f32[1,8,128]{2,1,0:T(8,128)S(1)}, u32[]{:S(2)}, u32[]{:S(2)}) collective-permute-start(f32[1,8,128]{2,1,0:T(8,128)S(1)} %get-tuple-element.124), channel_id=1, source_target_pairs={{16,0},{32,16},{48,32},{64,48},{80,64},{96,80},{112,96},{128,112},... | collective-permute-start | bytes 12296 | tf_op jit(solution)/shard_map/ppermute | solution.py:19
  308.4 4.3 collective-permute-start.69
  315.5 7.2 %collective-permute-start.71 = (f32[1,8,128]{2,1,0:T(8,128)S(1)}, f32[1,8,128]{2,1,0:T(8,128)S(1)}, u32[]{:S(2)}, u32[]{:S(2)}) collective-permute-start(f32[1,8,128]{2,1,0:T(8,128)S(1)} %get-tuple-element.120), channel_id=1, source_target_pairs={{16,0},{32,16},{48,32},{64,48},{80,64},{96,80},{112,96},{128,112},... | collective-permute-start | bytes 12296 | tf_op jit(solution)/shard_map/ppermute | solution.py:19
  323.5 4.3 collective-permute-start.73
  330.7 7.2 %collective-permute-start.75 = (f32[1,8,128]{2,1,0:T(8,128)S(1)}, f32[1,8,128]{2,1,0:T(8,128)S(1)}, u32[]{:S(2)}, u32[]{:S(2)}) collective-permute-start(f32[1,8,128]{2,1,0:T(8,128)S(1)} %get-tuple-element.116), channel_id=1, source_target_pairs={{16,0},{32,16},{48,32},{64,48},{80,64},{96,80},{112,96},{128,112},... | collective-permute-start | bytes 12296 | tf_op jit(solution)/shard_map/ppermute | solution.py:19
  338.7 4.3 collective-permute-start.77
  343.9 1.9 collective-permute-start.78
  345.8 7.2 %collective-permute-start.79 = (f32[1,8,128]{2,1,0:T(8,128)S(1)}, f32[1,8,128]{2,1,0:T(8,128)S(1)}, u32[]{:S(2)}, u32[]{:S(2)}) collective-permute-start(f32[1,8,128]{2,1,0:T(8,128)S(1)} %get-tuple-element.114), channel_id=1, source_target_pairs={{16,0},{32,16},{48,32},{64,48},{80,64},{96,80},{112,96},{128,112},... | collective-permute-start | bytes 12296 | tf_op jit(solution)/shard_map/ppermute | solution.py:19
  353.8 4.3 collective-permute-start.81
  359.0 4.0 broadcast_in_dim.5
  363.0 6.9 %reshape.131 = f32[8,16,256]{2,1,0:T(8,128)S(1)} reshape(f32[4,2,8,2,128,2]{5,4,3,2,1,0:T(8,128)} %broadcast_in_dim.5) | data formatting | bytes 262144 | tf_op jit(solution)/shard_map/reshape | solution.py:61
  371.9 7.2 %collective-permute-start.83 = (f32[1,16,256]{2,1,0:T(8,128)S(1)}, f32[1,16,256]{2,1,0:T(8,128)S(1)}, u32[]{:S(2)}, u32[]{:S(2)}) collective-permute-start(f32[1,16,256]{2,1,0:T(8,128)S(1)} %get-tuple-element.72), channel_id=1, source_target_pairs={{16,0},{32,16},{48,32},{64,48},{80,64},{96,80},{112,96},{128,112},... | collective-permute-start | bytes 49160 | tf_op jit(solution)/shard_map/ppermute | solution.py:19
  380.0 4.3 collective-permute-start.85
  387.3 7.2 %collective-permute-start.87 = (f32[1,16,256]{2,1,0:T(8,128)S(1)}, f32[1,16,256]{2,1,0:T(8,128)S(1)}, u32[]{:S(2)}, u32[]{:S(2)}) collective-permute-start(f32[1,16,256]{2,1,0:T(8,128)S(1)} %get-tuple-element.68), channel_id=1, source_target_pairs={{16,0},{32,16},{48,32},{64,48},{80,64},{96,80},{112,96},{128,112},... | collective-permute-start | bytes 49160 | tf_op jit(solution)/shard_map/ppermute | solution.py:19
  395.4 4.4 %collective-permute-start.89 = (f32[10,1,256]{2,1,0:T(1,128)S(1)}, f32[10,1,256]{2,1,0:T(1,128)S(1)}, u32[]{:S(2)}, u32[]{:S(2)}) collective-permute-start(f32[10,1,256]{2,1,0:T(1,128)S(1)} %get-tuple-element.46), channel_id=1, source_target_pairs={{1,0},{2,1},{3,2},{4,3},{5,4},{6,5},{7,6},{8,7},{9,8},{10,9},{11,1... | collective-permute-start | bytes 30728 | tf_op jit(solution)/shard_map/ppermute | solution.py:19
  402.8 7.2 %collective-permute-start.91 = (f32[1,16,256]{2,1,0:T(8,128)S(1)}, f32[1,16,256]{2,1,0:T(8,128)S(1)}, u32[]{:S(2)}, u32[]{:S(2)}) collective-permute-start(f32[1,16,256]{2,1,0:T(8,128)S(1)} %get-tuple-element.64), channel_id=1, source_target_pairs={{16,0},{32,16},{48,32},{64,48},{80,64},{96,80},{112,96},{128,112},... | collective-permute-start | bytes 49160 | tf_op jit(solution)/shard_map/ppermute | solution.py:19
  410.9 4.4 %collective-permute-start.93 = (f32[10,1,256]{2,1,0:T(1,128)S(1)}, f32[10,1,256]{2,1,0:T(1,128)S(1)}, u32[]{:S(2)}, u32[]{:S(2)}) collective-permute-start(f32[10,1,256]{2,1,0:T(1,128)S(1)} %get-tuple-element.44), channel_id=1, source_target_pairs={{1,0},{2,1},{3,2},{4,3},{5,4},{6,5},{7,6},{8,7},{9,8},{10,9},{11,1... | collective-permute-start | bytes 30728 | tf_op jit(solution)/shard_map/ppermute | solution.py:19
  416.4 1.9 collective-permute-start.94
  418.3 7.2 %collective-permute-start.95 = (f32[1,16,256]{2,1,0:T(8,128)S(1)}, f32[1,16,256]{2,1,0:T(8,128)S(1)}, u32[]{:S(2)}, u32[]{:S(2)}) collective-permute-start(f32[1,16,256]{2,1,0:T(8,128)S(1)} %get-tuple-element.62), channel_id=1, source_target_pairs={{16,0},{32,16},{48,32},{64,48},{80,64},{96,80},{112,96},{128,112},... | collective-permute-start | bytes 49160 | tf_op jit(solution)/shard_map/ppermute | solution.py:19
  426.4 4.4 %collective-permute-start.97 = (f32[10,1,256]{2,1,0:T(1,128)S(1)}, f32[10,1,256]{2,1,0:T(1,128)S(1)}, u32[]{:S(2)}, u32[]{:S(2)}) collective-permute-start(f32[10,1,256]{2,1,0:T(1,128)S(1)} %get-tuple-element.42), channel_id=1, source_target_pairs={{1,0},{2,1},{3,2},{4,3},{5,4},{6,5},{7,6},{8,7},{9,8},{10,9},{11,1... | collective-permute-start | bytes 30728 | tf_op jit(solution)/shard_map/ppermute | solution.py:19
  (312 shorter events, 88.9 us)
Async XLA Ops:
  1.4 39.5 %collective-permute-start.1 = (f32[1,16,256]{2,1,0:T(8,128)}, f32[1,16,256]{2,1,0:T(8,128)S(1)}, u32[]{:S(2)}, u32[]{:S(2)}) collective-permute-start(f32[1,16,256]{2,1,0:T(8,128)} %slice.870), channel_id=1, source_target_pairs={{16,0},{32,16},{48,32},{64,48},{80,64},{96,80},{112,96},{128,112},... | collective-permute-start | bytes 49160 | tf_op jit(solution)/shard_map/ppermute | solution.py:27
  10.4 30.5 %collective-permute-start.4 = (f32[8,1,256]{2,1,0:T(1,128)S(1)}, f32[8,1,256]{2,1,0:T(1,128)S(1)}, u32[]{:S(2)}, u32[]{:S(2)}) collective-permute-start(f32[8,1,256]{2,1,0:T(1,128)S(1)} %slice.876), channel_id=1, source_target_pairs={{1,0},{2,1},{3,2},{4,3},{5,4},{6,5},{7,6},{8,7},{9,8},{10,9},{11,1... | collective-permute-start | bytes 24584 | tf_op jit(solution)/shard_map/ppermute | solution.py:27
  12.1 17.5 %collective-permute-start = (f32[1,16,256]{2,1,0:T(8,128)S(1)}, f32[1,16,256]{2,1,0:T(8,128)S(1)}, u32[]{:S(2)}, u32[]{:S(2)}) collective-permute-start(f32[1,16,256]{2,1,0:T(8,128)S(1)} %get-tuple-element.92), channel_id=1, source_target_pairs={{0,16},{16,32},{32,48},{48,64},{64,80},{80,96},{96,112},{112,128},... | collective-permute-start | bytes 49160 | tf_op jit(solution)/shard_map/ppermute | solution.py:16
  15.4 14.2 %collective-permute-start.2 = (f32[1,16,256]{2,1,0:T(8,128)S(1)}, f32[1,16,256]{2,1,0:T(8,128)S(1)}, u32[]{:S(2)}, u32[]{:S(2)}) collective-permute-start(f32[1,16,256]{2,1,0:T(8,128)S(1)} %get-tuple-element.91), channel_id=1, source_target_pairs={{16,0},{32,16},{48,32},{64,48},{80,64},{96,80},{112,96},{128,112},... | collective-permute-start | bytes 49160 | tf_op jit(solution)/shard_map/ppermute | solution.py:19
  29.6 11.3 %collective-permute-start.3 = (f32[10,1,256]{2,1,0:T(1,128)S(1)}, f32[10,1,256]{2,1,0:T(1,128)S(1)}, u32[]{:S(2)}, u32[]{:S(2)}) collective-permute-start(f32[10,1,256]{2,1,0:T(1,128)S(1)} %get-tuple-element.57), channel_id=1, source_target_pairs={{0,1},{1,2},{2,3},{3,4},{4,5},{5,6},{6,7},{7,8},{8,9},{9,10},{10,1... | collective-permute-start | bytes 30728 | tf_op jit(solution)/shard_map/ppermute | solution.py:16
  32.2 8.7 %collective-permute-start.5 = (f32[10,1,256]{2,1,0:T(1,128)S(1)}, f32[10,1,256]{2,1,0:T(1,128)S(1)}, u32[]{:S(2)}, u32[]{:S(2)}) collective-permute-start(f32[10,1,256]{2,1,0:T(1,128)S(1)} %get-tuple-element.58), channel_id=1, source_target_pairs={{1,0},{2,1},{3,2},{4,3},{5,4},{6,5},{7,6},{8,7},{9,8},{10,9},{11,1... | collective-permute-start | bytes 30728 | tf_op jit(solution)/shard_map/ppermute | solution.py:19
  41.9 9.3 %collective-permute-start.6 = (f32[1,16,256]{2,1,0:T(8,128)S(1)}, f32[1,16,256]{2,1,0:T(8,128)S(1)}, u32[]{:S(2)}, u32[]{:S(2)}) collective-permute-start(f32[1,16,256]{2,1,0:T(8,128)S(1)} %get-tuple-element.87), channel_id=1, source_target_pairs={{0,16},{16,32},{32,48},{48,64},{64,80},{80,96},{96,112},{112,128},... | collective-permute-start | bytes 49160 | tf_op jit(solution)/shard_map/ppermute | solution.py:16
  43.9 7.5 %collective-permute-start.7 = (f32[1,16,256]{2,1,0:T(8,128)S(1)}, f32[1,16,256]{2,1,0:T(8,128)S(1)}, u32[]{:S(2)}, u32[]{:S(2)}) collective-permute-start(f32[1,16,256]{2,1,0:T(8,128)S(1)} %get-tuple-element.88), channel_id=1, source_target_pairs={{16,0},{32,16},{48,32},{64,48},{80,64},{96,80},{112,96},{128,112},... | collective-permute-start | bytes 49160 | tf_op jit(solution)/shard_map/ppermute | solution.py:19
  56.6 24.3 %collective-permute-start.10 = (f32[1,16,256]{2,1,0:T(8,128)S(1)}, f32[1,16,256]{2,1,0:T(8,128)S(1)}, u32[]{:S(2)}, u32[]{:S(2)}) collective-permute-start(f32[1,16,256]{2,1,0:T(8,128)S(1)} %get-tuple-element.83), channel_id=1, source_target_pairs={{0,16},{16,32},{32,48},{48,64},{64,80},{80,96},{96,112},{112,128},... | collective-permute-start | bytes 49160 | tf_op jit(solution)/shard_map/ppermute | solution.py:16
  58.5 22.4 %collective-permute-start.11 = (f32[1,16,256]{2,1,0:T(8,128)S(1)}, f32[1,16,256]{2,1,0:T(8,128)S(1)}, u32[]{:S(2)}, u32[]{:S(2)}) collective-permute-start(f32[1,16,256]{2,1,0:T(8,128)S(1)} %get-tuple-element.84), channel_id=1, source_target_pairs={{16,0},{32,16},{48,32},{64,48},{80,64},{96,80},{112,96},{128,112},... | collective-permute-start | bytes 49160 | tf_op jit(solution)/shard_map/ppermute | solution.py:19
  85.8 9.9 %collective-permute-start.14 = (f32[1,16,256]{2,1,0:T(8,128)S(1)}, f32[1,16,256]{2,1,0:T(8,128)S(1)}, u32[]{:S(2)}, u32[]{:S(2)}) collective-permute-start(f32[1,16,256]{2,1,0:T(8,128)S(1)} %get-tuple-element.81), channel_id=1, source_target_pairs={{0,16},{16,32},{32,48},{48,64},{64,80},{80,96},{96,112},{112,128},... | collective-permute-start | bytes 49160 | tf_op jit(solution)/shard_map/ppermute | solution.py:16
  87.7 7.9 %collective-permute-start.15 = (f32[1,16,256]{2,1,0:T(8,128)S(1)}, f32[1,16,256]{2,1,0:T(8,128)S(1)}, u32[]{:S(2)}, u32[]{:S(2)}) collective-permute-start(f32[1,16,256]{2,1,0:T(8,128)S(1)} %get-tuple-element.82), channel_id=1, source_target_pairs={{16,0},{32,16},{48,32},{64,48},{80,64},{96,80},{112,96},{128,112},... | collective-permute-start | bytes 49160 | tf_op jit(solution)/shard_map/ppermute | solution.py:19
  101.0 9.4 %collective-permute-start.18 = (f32[1,16,256]{2,1,0:T(8,128)S(1)}, f32[1,16,256]{2,1,0:T(8,128)S(1)}, u32[]{:S(2)}, u32[]{:S(2)}) collective-permute-start(f32[1,16,256]{2,1,0:T(8,128)S(1)} %get-tuple-element.77), channel_id=1, source_target_pairs={{0,16},{16,32},{32,48},{48,64},{64,80},{80,96},{96,112},{112,128},... | collective-permute-start | bytes 49160 | tf_op jit(solution)/shard_map/ppermute | solution.py:16
  102.9 8.1 %collective-permute-start.19 = (f32[1,16,256]{2,1,0:T(8,128)S(1)}, f32[1,16,256]{2,1,0:T(8,128)S(1)}, u32[]{:S(2)}, u32[]{:S(2)}) collective-permute-start(f32[1,16,256]{2,1,0:T(8,128)S(1)} %get-tuple-element.78), channel_id=1, source_target_pairs={{16,0},{32,16},{48,32},{64,48},{80,64},{96,80},{112,96},{128,112},... | collective-permute-start | bytes 49160 | tf_op jit(solution)/shard_map/ppermute | solution.py:19
  111.1 5.2 %collective-permute-start.21 = (f32[10,1,256]{2,1,0:T(1,128)S(1)}, f32[10,1,256]{2,1,0:T(1,128)S(1)}, u32[]{:S(2)}, u32[]{:S(2)}) collective-permute-start(f32[10,1,256]{2,1,0:T(1,128)S(1)} %get-tuple-element.50), channel_id=1, source_target_pairs={{1,0},{2,1},{3,2},{4,3},{5,4},{6,5},{7,6},{8,7},{9,8},{10,9},{11,1... | collective-permute-start | bytes 30728 | tf_op jit(solution)/shard_map/ppermute | solution.py:19
  130.3 9.6 %collective-permute-start.22 = (f32[1,8,128]{2,1,0:T(8,128)S(1)}, f32[1,8,128]{2,1,0:T(8,128)S(1)}, u32[]{:S(2)}, u32[]{:S(2)}) collective-permute-start(f32[1,8,128]{2,1,0:T(8,128)S(1)} %get-tuple-element.141), channel_id=1, source_target_pairs={{0,16},{16,32},{32,48},{48,64},{64,80},{80,96},{96,112},{112,128},... | collective-permute-start | bytes 12296 | tf_op jit(solution)/shard_map/ppermute | solution.py:16
  132.2 8.0 %collective-permute-start.23 = (f32[1,8,128]{2,1,0:T(8,128)S(1)}, f32[1,8,128]{2,1,0:T(8,128)S(1)}, u32[]{:S(2)}, u32[]{:S(2)}) collective-permute-start(f32[1,8,128]{2,1,0:T(8,128)S(1)} %get-tuple-element.142), channel_id=1, source_target_pairs={{16,0},{32,16},{48,32},{64,48},{80,64},{96,80},{112,96},{128,112},... | collective-permute-start | bytes 12296 | tf_op jit(solution)/shard_map/ppermute | solution.py:19
  140.2 5.2 %collective-permute-start.25 = (f32[6,1,128]{2,1,0:T(1,128)S(1)}, f32[6,1,128]{2,1,0:T(1,128)S(1)}, u32[]{:S(2)}, u32[]{:S(2)}) collective-permute-start(f32[6,1,128]{2,1,0:T(1,128)S(1)} %get-tuple-element.110), channel_id=1, source_target_pairs={{1,0},{2,1},{3,2},{4,3},{5,4},{6,5},{7,6},{8,7},{9,8},{10,9},{11,1... | collective-permute-start | bytes 9224 | tf_op jit(solution)/shard_map/ppermute | solution.py:19
  145.5 9.5 %collective-permute-start.26 = (f32[1,8,128]{2,1,0:T(8,128)S(1)}, f32[1,8,128]{2,1,0:T(8,128)S(1)}, u32[]{:S(2)}, u32[]{:S(2)}) collective-permute-start(f32[1,8,128]{2,1,0:T(8,128)S(1)} %get-tuple-element.137), channel_id=1, source_target_pairs={{0,16},{16,32},{32,48},{48,64},{64,80},{80,96},{96,112},{112,128},... | collective-permute-start | bytes 12296 | tf_op jit(solution)/shard_map/ppermute | solution.py:16
  147.4 8.0 %collective-permute-start.27 = (f32[1,8,128]{2,1,0:T(8,128)S(1)}, f32[1,8,128]{2,1,0:T(8,128)S(1)}, u32[]{:S(2)}, u32[]{:S(2)}) collective-permute-start(f32[1,8,128]{2,1,0:T(8,128)S(1)} %get-tuple-element.138), channel_id=1, source_target_pairs={{16,0},{32,16},{48,32},{64,48},{80,64},{96,80},{112,96},{128,112},... | collective-permute-start | bytes 12296 | tf_op jit(solution)/shard_map/ppermute | solution.py:19
  155.4 5.1 %collective-permute-start.29 = (f32[6,1,128]{2,1,0:T(1,128)S(1)}, f32[6,1,128]{2,1,0:T(1,128)S(1)}, u32[]{:S(2)}, u32[]{:S(2)}) collective-permute-start(f32[6,1,128]{2,1,0:T(1,128)S(1)} %get-tuple-element.108), channel_id=1, source_target_pairs={{1,0},{2,1},{3,2},{4,3},{5,4},{6,5},{7,6},{8,7},{9,8},{10,9},{11,1... | collective-permute-start | bytes 9224 | tf_op jit(solution)/shard_map/ppermute | solution.py:19
  160.6 9.5 %collective-permute-start.30 = (f32[1,8,128]{2,1,0:T(8,128)S(1)}, f32[1,8,128]{2,1,0:T(8,128)S(1)}, u32[]{:S(2)}, u32[]{:S(2)}) collective-permute-start(f32[1,8,128]{2,1,0:T(8,128)S(1)} %get-tuple-element.135), channel_id=1, source_target_pairs={{0,16},{16,32},{32,48},{48,64},{64,80},{80,96},{96,112},{112,128},... | collective-permute-start | bytes 12296 | tf_op jit(solution)/shard_map/ppermute | solution.py:16
  162.6 8.0 %collective-permute-start.31 = (f32[1,8,128]{2,1,0:T(8,128)S(1)}, f32[1,8,128]{2,1,0:T(8,128)S(1)}, u32[]{:S(2)}, u32[]{:S(2)}) collective-permute-start(f32[1,8,128]{2,1,0:T(8,128)S(1)} %get-tuple-element.136), channel_id=1, source_target_pairs={{16,0},{32,16},{48,32},{64,48},{80,64},{96,80},{112,96},{128,112},... | collective-permute-start | bytes 12296 | tf_op jit(solution)/shard_map/ppermute | solution.py:19
  170.6 5.1 %collective-permute-start.33 = (f32[6,1,128]{2,1,0:T(1,128)S(1)}, f32[6,1,128]{2,1,0:T(1,128)S(1)}, u32[]{:S(2)}, u32[]{:S(2)}) collective-permute-start(f32[6,1,128]{2,1,0:T(1,128)S(1)} %get-tuple-element.106), channel_id=1, source_target_pairs={{1,0},{2,1},{3,2},{4,3},{5,4},{6,5},{7,6},{8,7},{9,8},{10,9},{11,1... | collective-permute-start | bytes 9224 | tf_op jit(solution)/shard_map/ppermute | solution.py:19
  175.8 10.3 %collective-permute-start.34 = (f32[1,8,128]{2,1,0:T(8,128)S(1)}, f32[1,8,128]{2,1,0:T(8,128)S(1)}, u32[]{:S(2)}, u32[]{:S(2)}) collective-permute-start(f32[1,8,128]{2,1,0:T(8,128)S(1)} %get-tuple-element.131), channel_id=1, source_target_pairs={{0,16},{16,32},{32,48},{48,64},{64,80},{80,96},{96,112},{112,128},... | collective-permute-start | bytes 12296 | tf_op jit(solution)/shard_map/ppermute | solution.py:16
  177.7 8.4 %collective-permute-start.35 = (f32[1,8,128]{2,1,0:T(8,128)S(1)}, f32[1,8,128]{2,1,0:T(8,128)S(1)}, u32[]{:S(2)}, u32[]{:S(2)}) collective-permute-start(f32[1,8,128]{2,1,0:T(8,128)S(1)} %get-tuple-element.132), channel_id=1, source_target_pairs={{16,0},{32,16},{48,32},{64,48},{80,64},{96,80},{112,96},{128,112},... | collective-permute-start | bytes 12296 | tf_op jit(solution)/shard_map/ppermute | solution.py:19
  192.1 9.2 %collective-permute-start.38 = (f32[1,4,64]{2,1,0:T(4,128)S(1)}, f32[1,4,64]{2,1,0:T(4,128)S(1)}, u32[]{:S(2)}, u32[]{:S(2)}) collective-permute-start(f32[1,4,64]{2,1,0:T(4,128)S(1)} %get-tuple-element.183), channel_id=1, source_target_pairs={{0,16},{16,32},{32,48},{48,64},{64,80},{80,96},{96,112},{112,128},... | collective-permute-start | bytes 3080 | tf_op jit(solution)/shard_map/ppermute | solution.py:16
  194.0 8.0 %collective-permute-start.39 = (f32[1,4,64]{2,1,0:T(4,128)S(1)}, f32[1,4,64]{2,1,0:T(4,128)S(1)}, u32[]{:S(2)}, u32[]{:S(2)}) collective-permute-start(f32[1,4,64]{2,1,0:T(4,128)S(1)} %get-tuple-element.184), channel_id=1, source_target_pairs={{16,0},{32,16},{48,32},{64,48},{80,64},{96,80},{112,96},{128,112},... | collective-permute-start | bytes 3080 | tf_op jit(solution)/shard_map/ppermute | solution.py:19
  202.0 5.1 %collective-permute-start.41 = (f32[4,1,64]{2,1,0:T(1,128)S(1)}, f32[4,1,64]{2,1,0:T(1,128)S(1)}, u32[]{:S(2)}, u32[]{:S(2)}) collective-permute-start(f32[4,1,64]{2,1,0:T(1,128)S(1)} %get-tuple-element.158), channel_id=1, source_target_pairs={{1,0},{2,1},{3,2},{4,3},{5,4},{6,5},{7,6},{8,7},{9,8},{10,9},{11,1... | collective-permute-start | bytes 3080 | tf_op jit(solution)/shard_map/ppermute | solution.py:19
  207.2 9.2 %collective-permute-start.42 = (f32[1,4,64]{2,1,0:T(4,128)S(1)}, f32[1,4,64]{2,1,0:T(4,128)S(1)}, u32[]{:S(2)}, u32[]{:S(2)}) collective-permute-start(f32[1,4,64]{2,1,0:T(4,128)S(1)} %get-tuple-element.179), channel_id=1, source_target_pairs={{0,16},{16,32},{32,48},{48,64},{64,80},{80,96},{96,112},{112,128},... | collective-permute-start | bytes 3080 | tf_op jit(solution)/shard_map/ppermute | solution.py:16
  209.1 8.0 %collective-permute-start.43 = (f32[1,4,64]{2,1,0:T(4,128)S(1)}, f32[1,4,64]{2,1,0:T(4,128)S(1)}, u32[]{:S(2)}, u32[]{:S(2)}) collective-permute-start(f32[1,4,64]{2,1,0:T(4,128)S(1)} %get-tuple-element.180), channel_id=1, source_target_pairs={{16,0},{32,16},{48,32},{64,48},{80,64},{96,80},{112,96},{128,112},... | collective-permute-start | bytes 3080 | tf_op jit(solution)/shard_map/ppermute | solution.py:19
  222.3 9.2 %collective-permute-start.46 = (f32[1,4,64]{2,1,0:T(4,128)S(1)}, f32[1,4,64]{2,1,0:T(4,128)S(1)}, u32[]{:S(2)}, u32[]{:S(2)}) collective-permute-start(f32[1,4,64]{2,1,0:T(4,128)S(1)} %get-tuple-element.175), channel_id=1, source_target_pairs={{0,16},{16,32},{32,48},{48,64},{64,80},{80,96},{96,112},{112,128},... | collective-permute-start | bytes 3080 | tf_op jit(solution)/shard_map/ppermute | solution.py:16
  224.2 8.0 %collective-permute-start.47 = (f32[1,4,64]{2,1,0:T(4,128)S(1)}, f32[1,4,64]{2,1,0:T(4,128)S(1)}, u32[]{:S(2)}, u32[]{:S(2)}) collective-permute-start(f32[1,4,64]{2,1,0:T(4,128)S(1)} %get-tuple-element.176), channel_id=1, source_target_pairs={{16,0},{32,16},{48,32},{64,48},{80,64},{96,80},{112,96},{128,112},... | collective-permute-start | bytes 3080 | tf_op jit(solution)/shard_map/ppermute | solution.py:19
  237.4 9.2 %collective-permute-start.50 = (f32[1,4,64]{2,1,0:T(4,128)S(1)}, f32[1,4,64]{2,1,0:T(4,128)S(1)}, u32[]{:S(2)}, u32[]{:S(2)}) collective-permute-start(f32[1,4,64]{2,1,0:T(4,128)S(1)} %get-tuple-element.171), channel_id=1, source_target_pairs={{0,16},{16,32},{32,48},{48,64},{64,80},{80,96},{96,112},{112,128},... | collective-permute-start | bytes 3080 | tf_op jit(solution)/shard_map/ppermute | solution.py:16
  239.3 8.0 %collective-permute-start.51 = (f32[1,4,64]{2,1,0:T(4,128)S(1)}, f32[1,4,64]{2,1,0:T(4,128)S(1)}, u32[]{:S(2)}, u32[]{:S(2)}) collective-permute-start(f32[1,4,64]{2,1,0:T(4,128)S(1)} %get-tuple-element.172), channel_id=1, source_target_pairs={{16,0},{32,16},{48,32},{64,48},{80,64},{96,80},{112,96},{128,112},... | collective-permute-start | bytes 3080 | tf_op jit(solution)/shard_map/ppermute | solution.py:19
  252.5 9.2 %collective-permute-start.54 = (f32[1,4,64]{2,1,0:T(4,128)S(1)}, f32[1,4,64]{2,1,0:T(4,128)S(1)}, u32[]{:S(2)}, u32[]{:S(2)}) collective-permute-start(f32[1,4,64]{2,1,0:T(4,128)S(1)} %get-tuple-element.167), channel_id=1, source_target_pairs={{0,16},{16,32},{32,48},{48,64},{64,80},{80,96},{96,112},{112,128},... | collective-permute-start | bytes 3080 | tf_op jit(solution)/shard_map/ppermute | solution.py:16
  254.4 8.0 %collective-permute-start.55 = (f32[1,4,64]{2,1,0:T(4,128)S(1)}, f32[1,4,64]{2,1,0:T(4,128)S(1)}, u32[]{:S(2)}, u32[]{:S(2)}) collective-permute-start(f32[1,4,64]{2,1,0:T(4,128)S(1)} %get-tuple-element.168), channel_id=1, source_target_pairs={{16,0},{32,16},{48,32},{64,48},{80,64},{96,80},{112,96},{128,112},... | collective-permute-start | bytes 3080 | tf_op jit(solution)/shard_map/ppermute | solution.py:19
  267.6 9.2 %collective-permute-start.58 = (f32[1,4,64]{2,1,0:T(4,128)S(1)}, f32[1,4,64]{2,1,0:T(4,128)S(1)}, u32[]{:S(2)}, u32[]{:S(2)}) collective-permute-start(f32[1,4,64]{2,1,0:T(4,128)S(1)} %get-tuple-element.163), channel_id=1, source_target_pairs={{0,16},{16,32},{32,48},{48,64},{64,80},{80,96},{96,112},{112,128},... | collective-permute-start | bytes 3080 | tf_op jit(solution)/shard_map/ppermute | solution.py:16
  269.5 8.0 %collective-permute-start.59 = (f32[1,4,64]{2,1,0:T(4,128)S(1)}, f32[1,4,64]{2,1,0:T(4,128)S(1)}, u32[]{:S(2)}, u32[]{:S(2)}) collective-permute-start(f32[1,4,64]{2,1,0:T(4,128)S(1)} %get-tuple-element.164), channel_id=1, source_target_pairs={{16,0},{32,16},{48,32},{64,48},{80,64},{96,80},{112,96},{128,112},... | collective-permute-start | bytes 3080 | tf_op jit(solution)/shard_map/ppermute | solution.py:19
  282.7 9.2 %collective-permute-start.62 = (f32[1,4,64]{2,1,0:T(4,128)S(1)}, f32[1,4,64]{2,1,0:T(4,128)S(1)}, u32[]{:S(2)}, u32[]{:S(2)}) collective-permute-start(f32[1,4,64]{2,1,0:T(4,128)S(1)} %get-tuple-element.161), channel_id=1, source_target_pairs={{0,16},{16,32},{32,48},{48,64},{64,80},{80,96},{96,112},{112,128},... | collective-permute-start | bytes 3080 | tf_op jit(solution)/shard_map/ppermute | solution.py:16
  284.6 8.0 %collective-permute-start.63 = (f32[1,4,64]{2,1,0:T(4,128)S(1)}, f32[1,4,64]{2,1,0:T(4,128)S(1)}, u32[]{:S(2)}, u32[]{:S(2)}) collective-permute-start(f32[1,4,64]{2,1,0:T(4,128)S(1)} %get-tuple-element.162), channel_id=1, source_target_pairs={{16,0},{32,16},{48,32},{64,48},{80,64},{96,80},{112,96},{128,112},... | collective-permute-start | bytes 3080 | tf_op jit(solution)/shard_map/ppermute | solution.py:19
  298.5 9.2 %collective-permute-start.66 = (f32[1,8,128]{2,1,0:T(8,128)S(1)}, f32[1,8,128]{2,1,0:T(8,128)S(1)}, u32[]{:S(2)}, u32[]{:S(2)}) collective-permute-start(f32[1,8,128]{2,1,0:T(8,128)S(1)} %get-tuple-element.123), channel_id=1, source_target_pairs={{0,16},{16,32},{32,48},{48,64},{64,80},{80,96},{96,112},{112,128},... | collective-permute-start | bytes 12296 | tf_op jit(solution)/shard_map/ppermute | solution.py:16
  300.4 8.0 %collective-permute-start.67 = (f32[1,8,128]{2,1,0:T(8,128)S(1)}, f32[1,8,128]{2,1,0:T(8,128)S(1)}, u32[]{:S(2)}, u32[]{:S(2)}) collective-permute-start(f32[1,8,128]{2,1,0:T(8,128)S(1)} %get-tuple-element.124), channel_id=1, source_target_pairs={{16,0},{32,16},{48,32},{64,48},{80,64},{96,80},{112,96},{128,112},... | collective-permute-start | bytes 12296 | tf_op jit(solution)/shard_map/ppermute | solution.py:19
  313.6 9.2 %collective-permute-start.70 = (f32[1,8,128]{2,1,0:T(8,128)S(1)}, f32[1,8,128]{2,1,0:T(8,128)S(1)}, u32[]{:S(2)}, u32[]{:S(2)}) collective-permute-start(f32[1,8,128]{2,1,0:T(8,128)S(1)} %get-tuple-element.119), channel_id=1, source_target_pairs={{0,16},{16,32},{32,48},{48,64},{64,80},{80,96},{96,112},{112,128},... | collective-permute-start | bytes 12296 | tf_op jit(solution)/shard_map/ppermute | solution.py:16
  315.5 8.0 %collective-permute-start.71 = (f32[1,8,128]{2,1,0:T(8,128)S(1)}, f32[1,8,128]{2,1,0:T(8,128)S(1)}, u32[]{:S(2)}, u32[]{:S(2)}) collective-permute-start(f32[1,8,128]{2,1,0:T(8,128)S(1)} %get-tuple-element.120), channel_id=1, source_target_pairs={{16,0},{32,16},{48,32},{64,48},{80,64},{96,80},{112,96},{128,112},... | collective-permute-start | bytes 12296 | tf_op jit(solution)/shard_map/ppermute | solution.py:19
  323.5 5.1 %collective-permute-start.73 = (f32[6,1,128]{2,1,0:T(1,128)S(1)}, f32[6,1,128]{2,1,0:T(1,128)S(1)}, u32[]{:S(2)}, u32[]{:S(2)}) collective-permute-start(f32[6,1,128]{2,1,0:T(1,128)S(1)} %get-tuple-element.100), channel_id=1, source_target_pairs={{1,0},{2,1},{3,2},{4,3},{5,4},{6,5},{7,6},{8,7},{9,8},{10,9},{11,1... | collective-permute-start | bytes 9224 | tf_op jit(solution)/shard_map/ppermute | solution.py:19
  328.7 9.2 %collective-permute-start.74 = (f32[1,8,128]{2,1,0:T(8,128)S(1)}, f32[1,8,128]{2,1,0:T(8,128)S(1)}, u32[]{:S(2)}, u32[]{:S(2)}) collective-permute-start(f32[1,8,128]{2,1,0:T(8,128)S(1)} %get-tuple-element.115), channel_id=1, source_target_pairs={{0,16},{16,32},{32,48},{48,64},{64,80},{80,96},{96,112},{112,128},... | collective-permute-start | bytes 12296 | tf_op jit(solution)/shard_map/ppermute | solution.py:16
  330.7 8.0 %collective-permute-start.75 = (f32[1,8,128]{2,1,0:T(8,128)S(1)}, f32[1,8,128]{2,1,0:T(8,128)S(1)}, u32[]{:S(2)}, u32[]{:S(2)}) collective-permute-start(f32[1,8,128]{2,1,0:T(8,128)S(1)} %get-tuple-element.116), channel_id=1, source_target_pairs={{16,0},{32,16},{48,32},{64,48},{80,64},{96,80},{112,96},{128,112},... | collective-permute-start | bytes 12296 | tf_op jit(solution)/shard_map/ppermute | solution.py:19
  338.7 5.1 %collective-permute-start.77 = (f32[6,1,128]{2,1,0:T(1,128)S(1)}, f32[6,1,128]{2,1,0:T(1,128)S(1)}, u32[]{:S(2)}, u32[]{:S(2)}) collective-permute-start(f32[6,1,128]{2,1,0:T(1,128)S(1)} %get-tuple-element.98), channel_id=1, source_target_pairs={{1,0},{2,1},{3,2},{4,3},{5,4},{6,5},{7,6},{8,7},{9,8},{10,9},{11,1... | collective-permute-start | bytes 9224 | tf_op jit(solution)/shard_map/ppermute | solution.py:19
  343.9 9.2 %collective-permute-start.78 = (f32[1,8,128]{2,1,0:T(8,128)S(1)}, f32[1,8,128]{2,1,0:T(8,128)S(1)}, u32[]{:S(2)}, u32[]{:S(2)}) collective-permute-start(f32[1,8,128]{2,1,0:T(8,128)S(1)} %get-tuple-element.113), channel_id=1, source_target_pairs={{0,16},{16,32},{32,48},{48,64},{64,80},{80,96},{96,112},{112,128},... | collective-permute-start | bytes 12296 | tf_op jit(solution)/shard_map/ppermute | solution.py:16
  345.8 8.0 %collective-permute-start.79 = (f32[1,8,128]{2,1,0:T(8,128)S(1)}, f32[1,8,128]{2,1,0:T(8,128)S(1)}, u32[]{:S(2)}, u32[]{:S(2)}) collective-permute-start(f32[1,8,128]{2,1,0:T(8,128)S(1)} %get-tuple-element.114), channel_id=1, source_target_pairs={{16,0},{32,16},{48,32},{64,48},{80,64},{96,80},{112,96},{128,112},... | collective-permute-start | bytes 12296 | tf_op jit(solution)/shard_map/ppermute | solution.py:19
  353.8 5.1 %collective-permute-start.81 = (f32[6,1,128]{2,1,0:T(1,128)S(1)}, f32[6,1,128]{2,1,0:T(1,128)S(1)}, u32[]{:S(2)}, u32[]{:S(2)}) collective-permute-start(f32[6,1,128]{2,1,0:T(1,128)S(1)} %get-tuple-element.96), channel_id=1, source_target_pairs={{1,0},{2,1},{3,2},{4,3},{5,4},{6,5},{7,6},{8,7},{9,8},{10,9},{11,1... | collective-permute-start | bytes 9224 | tf_op jit(solution)/shard_map/ppermute | solution.py:19
  370.0 9.2 %collective-permute-start.82 = (f32[1,16,256]{2,1,0:T(8,128)S(1)}, f32[1,16,256]{2,1,0:T(8,128)S(1)}, u32[]{:S(2)}, u32[]{:S(2)}) collective-permute-start(f32[1,16,256]{2,1,0:T(8,128)S(1)} %get-tuple-element.71), channel_id=1, source_target_pairs={{0,16},{16,32},{32,48},{48,64},{64,80},{80,96},{96,112},{112,128},... | collective-permute-start | bytes 49160 | tf_op jit(solution)/shard_map/ppermute | solution.py:16
  371.9 8.1 %collective-permute-start.83 = (f32[1,16,256]{2,1,0:T(8,128)S(1)}, f32[1,16,256]{2,1,0:T(8,128)S(1)}, u32[]{:S(2)}, u32[]{:S(2)}) collective-permute-start(f32[1,16,256]{2,1,0:T(8,128)S(1)} %get-tuple-element.72), channel_id=1, source_target_pairs={{16,0},{32,16},{48,32},{64,48},{80,64},{96,80},{112,96},{128,112},... | collective-permute-start | bytes 49160 | tf_op jit(solution)/shard_map/ppermute | solution.py:19
  380.0 5.1 %collective-permute-start.85 = (f32[10,1,256]{2,1,0:T(1,128)S(1)}, f32[10,1,256]{2,1,0:T(1,128)S(1)}, u32[]{:S(2)}, u32[]{:S(2)}) collective-permute-start(f32[10,1,256]{2,1,0:T(1,128)S(1)} %get-tuple-element.48), channel_id=1, source_target_pairs={{1,0},{2,1},{3,2},{4,3},{5,4},{6,5},{7,6},{8,7},{9,8},{10,9},{11,1... | collective-permute-start | bytes 30728 | tf_op jit(solution)/shard_map/ppermute | solution.py:19
  385.4 9.2 %collective-permute-start.86 = (f32[1,16,256]{2,1,0:T(8,128)S(1)}, f32[1,16,256]{2,1,0:T(8,128)S(1)}, u32[]{:S(2)}, u32[]{:S(2)}) collective-permute-start(f32[1,16,256]{2,1,0:T(8,128)S(1)} %get-tuple-element.67), channel_id=1, source_target_pairs={{0,16},{16,32},{32,48},{48,64},{64,80},{80,96},{96,112},{112,128},... | collective-permute-start | bytes 49160 | tf_op jit(solution)/shard_map/ppermute | solution.py:16
  387.3 8.1 %collective-permute-start.87 = (f32[1,16,256]{2,1,0:T(8,128)S(1)}, f32[1,16,256]{2,1,0:T(8,128)S(1)}, u32[]{:S(2)}, u32[]{:S(2)}) collective-permute-start(f32[1,16,256]{2,1,0:T(8,128)S(1)} %get-tuple-element.68), channel_id=1, source_target_pairs={{16,0},{32,16},{48,32},{64,48},{80,64},{96,80},{112,96},{128,112},... | collective-permute-start | bytes 49160 | tf_op jit(solution)/shard_map/ppermute | solution.py:19
  395.4 5.2 %collective-permute-start.89 = (f32[10,1,256]{2,1,0:T(1,128)S(1)}, f32[10,1,256]{2,1,0:T(1,128)S(1)}, u32[]{:S(2)}, u32[]{:S(2)}) collective-permute-start(f32[10,1,256]{2,1,0:T(1,128)S(1)} %get-tuple-element.46), channel_id=1, source_target_pairs={{1,0},{2,1},{3,2},{4,3},{5,4},{6,5},{7,6},{8,7},{9,8},{10,9},{11,1... | collective-permute-start | bytes 30728 | tf_op jit(solution)/shard_map/ppermute | solution.py:19
  400.9 9.2 %collective-permute-start.90 = (f32[1,16,256]{2,1,0:T(8,128)S(1)}, f32[1,16,256]{2,1,0:T(8,128)S(1)}, u32[]{:S(2)}, u32[]{:S(2)}) collective-permute-start(f32[1,16,256]{2,1,0:T(8,128)S(1)} %get-tuple-element.63), channel_id=1, source_target_pairs={{0,16},{16,32},{32,48},{48,64},{64,80},{80,96},{96,112},{112,128},... | collective-permute-start | bytes 49160 | tf_op jit(solution)/shard_map/ppermute | solution.py:16
  402.8 8.1 %collective-permute-start.91 = (f32[1,16,256]{2,1,0:T(8,128)S(1)}, f32[1,16,256]{2,1,0:T(8,128)S(1)}, u32[]{:S(2)}, u32[]{:S(2)}) collective-permute-start(f32[1,16,256]{2,1,0:T(8,128)S(1)} %get-tuple-element.64), channel_id=1, source_target_pairs={{16,0},{32,16},{48,32},{64,48},{80,64},{96,80},{112,96},{128,112},... | collective-permute-start | bytes 49160 | tf_op jit(solution)/shard_map/ppermute | solution.py:19
  410.9 5.2 %collective-permute-start.93 = (f32[10,1,256]{2,1,0:T(1,128)S(1)}, f32[10,1,256]{2,1,0:T(1,128)S(1)}, u32[]{:S(2)}, u32[]{:S(2)}) collective-permute-start(f32[10,1,256]{2,1,0:T(1,128)S(1)} %get-tuple-element.44), channel_id=1, source_target_pairs={{1,0},{2,1},{3,2},{4,3},{5,4},{6,5},{7,6},{8,7},{9,8},{10,9},{11,1... | collective-permute-start | bytes 30728 | tf_op jit(solution)/shard_map/ppermute | solution.py:19
  416.4 9.2 %collective-permute-start.94 = (f32[1,16,256]{2,1,0:T(8,128)S(1)}, f32[1,16,256]{2,1,0:T(8,128)S(1)}, u32[]{:S(2)}, u32[]{:S(2)}) collective-permute-start(f32[1,16,256]{2,1,0:T(8,128)S(1)} %get-tuple-element.61), channel_id=1, source_target_pairs={{0,16},{16,32},{32,48},{48,64},{64,80},{80,96},{96,112},{112,128},... | collective-permute-start | bytes 49160 | tf_op jit(solution)/shard_map/ppermute | solution.py:16
  418.3 8.1 %collective-permute-start.95 = (f32[1,16,256]{2,1,0:T(8,128)S(1)}, f32[1,16,256]{2,1,0:T(8,128)S(1)}, u32[]{:S(2)}, u32[]{:S(2)}) collective-permute-start(f32[1,16,256]{2,1,0:T(8,128)S(1)} %get-tuple-element.62), channel_id=1, source_target_pairs={{16,0},{32,16},{48,32},{64,48},{80,64},{96,80},{112,96},{128,112},... | collective-permute-start | bytes 49160 | tf_op jit(solution)/shard_map/ppermute | solution.py:19
  426.4 5.2 %collective-permute-start.97 = (f32[10,1,256]{2,1,0:T(1,128)S(1)}, f32[10,1,256]{2,1,0:T(1,128)S(1)}, u32[]{:S(2)}, u32[]{:S(2)}) collective-permute-start(f32[10,1,256]{2,1,0:T(1,128)S(1)} %get-tuple-element.42), channel_id=1, source_target_pairs={{1,0},{2,1},{3,2},{4,3},{5,4},{6,5},{7,6},{8,7},{9,8},{10,9},{11,1... | collective-permute-start | bytes 30728 | tf_op jit(solution)/shard_map/ppermute | solution.py:19
  (42 other events, 412.3 us)
where the time goes:
time: 436 us; the launch traced here: 432 us
  starting transfers between devices  334 us (77%)
  local copies, waits for them, and re-layouts  48.6 us (11%)
  waiting for transfers between devices  30.3 us (7%)
  other arithmetic  18.1 us (4%)
    ppermute x48, starting transfers between devices, extended(): lax.ppermute(lax.slice_in_dim(block, 0, width, axis=dim), axis, backward)  275 us
    ppermute x48, starting transfers between devices, extended(): lax.ppermute(lax.slice_in_dim(block, block.shape[dim] - width, None, axis...  50.2 us
    reshape x3, local copies, waits for them, and re-layouts, restrict_cells(): field.reshape(size_x // 2, 2, size_y // 2, 2, size_z // 2, 2)  20.6 us
    ppermute x48, waiting for transfers between devices, extended(): lax.ppermute(lax.slice_in_dim(block, 0, width, axis=dim), axis, backward)  17.4 us
    ppermute x48, waiting for transfers between devices, extended(): lax.ppermute(lax.slice_in_dim(block, block.shape[dim] - width, None, axis...  12.9 us
    ppermute x2, starting transfers between devices, passed_along(): return lax.ppermute(block, axis, route)  9.05 us
  transfers between devices with their start and end apart: 98, of which 66 were waited for; matrix products, arithmetic and copies ran while one was open for 8% of the time, Pallas kernels for 0%

commit v1 on v0

v1 whole, which is shorter than its diff:
```python
import jax
import jax.numpy as jnp
from jax import lax
from jax.experimental import pallas as pl
from jax.experimental.pallas import tpu as pltpu
from jax.sharding import PartitionSpec as P

SWEEPS = 4
COARSE_SWEEPS = 8
LANES = 128
HALF = 64
MESH = pl.DeviceIdType.MESH

NX0, NY0, HX0, HY0, YP0 = 8, 16, 5, 5, 26
NX1, NY1, HX1, HY1, YP1 = 4, 8, 6, 9, 26
NX2, NY2, HX2, HY2, YP2 = 2, 4, 10, 12, 28
ROWS0 = 472
ROWS1 = 416
ROWS2 = 616

DEPTH = 5
NEAR = [(-1, 0), (1, 0), (0, -1), (0, 1), (-1, -1), (-1, 1), (1, -1), (1, 1)]
WIDE = [(-2, 0), (2, 0), (-2, -1), (-2, 1), (2, -1), (2, 1)]
MIDS = NEAR + WIDE


def ball_offsets():
    offsets = []
    for i in range(-5, 6):
        for j in range(-3, 4):
            far_x = 2 * abs(i) - 1 if i else 0
            far_y = 4 * abs(j) - 3 if j else 0
            if (i, j) != (0, 0) and far_x + far_y <= (11 if i and j else 10):
                offsets.append((i, j))
    return offsets


BALL = ball_offsets()


def chebyshev_weights(sweeps):
    cheb_theta = 1.125
    cheb_delta = 0.875
    cheb_sigma = cheb_theta / cheb_delta
    rho_old = 1.0 / cheb_sigma
    weights = [(0.0, 1.0 / cheb_theta)]
    for sweep in range(1, sweeps):
        rho_new = 1.0 / (2.0 * cheb_sigma - rho_old)
        weights.append((rho_new * rho_old, 2.0 * rho_new / cheb_delta))
        rho_old = rho_new
    return weights


def row0(x, y):
    return (x + HX0) * YP0 + y + HY0


def row1(x, y):
    return (x + HX1) * YP1 + y + HY1


def row2(x, y):
    return (x + HX2) * YP2 + y + HY2


def lanes(shape):
    return lax.broadcasted_iota(jnp.int32, shape, len(shape) - 1)


def shift_down(v):
    return jnp.where(lanes(v.shape) < HALF, pltpu.roll(v, HALF + 1, 1), pltpu.roll(v, HALF, 1))


def shift_up(v):
    return jnp.where(lanes(v.shape) < HALF, pltpu.roll(v, HALF, 1), pltpu.roll(v, HALF - 1, 1))


def z_neighbours(values, level):
    if level == 0:
        return (shift_down(values[1]), values[0]), (values[1], shift_up(values[0]))
    if level == 1:
        return (shift_down(values[0]),), (shift_up(values[0]),)
    return (pltpu.roll(values[0], 1, 1),), (pltpu.roll(values[0], LANES - 1, 1),)


def z_ends(shape, level, half):
    at = lanes(shape)
    if level == 0:
        return (at == 0) if half == 0 else None, (at == LANES - 1) if half == 1 else None
    if level == 1:
        return at == 0, at == LANES - 1
    return (at % HALF) == 0, (at % HALF) == HALF - 1


def plane_loop(first, count, body):
    def pair(i, carry):
        body(first + 2 * i)
        body(first + 2 * i + 1)
        return carry

    lax.fori_loop(0, count // 2, pair, 0)


class Level:
    def __init__(self, number, halves, row, pitch, raw, coef, diag, rhs, update):
        self.number, self.halves, self.row, self.pitch = number, halves, row, pitch
        self.raw, self.coef, self.diag, self.rhs, self.update = raw, coef, diag, rhs, update
        self.scale = 0.25**number

    def faces(self, at, rows):
        n, raw = self.halves, self.raw
        take = lambda k, e, shift=0: raw[k * n + e, pl.ds(at + shift, rows), :]
        low_z = [take(3, e) for e in range(n)]
        _, high_z = z_neighbours(low_z, self.number)
        out = []
        for e in range(n):
            _, top = z_ends((rows, LANES), self.number, e)
            upper = high_z[e] if top is None else jnp.where(top, 0.0, high_z[e])
            faces = [take(1, e), take(1, e, self.pitch), take(2, e), take(2, e, 1), low_z[e], upper]
            total = (faces[0] + faces[1]) + (faces[2] + faces[3]) + (faces[4] + faces[5])
            out.append((faces, take(0, e) + self.scale * total))
        return out

    def own_diagonal(self, x, y, rows):
        return [d for _, d in self.faces(self.row(x, y), rows)]

    def build(self, first_x, count, first_y, rows, source=None):
        n = self.halves

        def body(x):
            at = self.row(x, first_y)
            for e, (faces, diagonal) in enumerate(self.faces(at, rows)):
                inverse = 1.0 / diagonal
                low, _ = z_ends((rows, LANES), self.number, e)
                if low is not None:
                    faces[4] = jnp.where(low, 0.0, faces[4])
                scaled = self.scale * inverse
                for c in range(6):
                    self.coef[c * n + e, pl.ds(at, rows), :] = faces[c] * scaled
                self.diag[e, pl.ds(at, rows), :] = diagonal
                if source is not None:
                    ref, base = source
                    self.rhs[e, pl.ds(at, rows), :] = ref[base + e, pl.ds(at, rows), :] * inverse

        plane_loop(first_x, count, body)

    def residual(self, src, at, rows):
        n = self.halves
        ref, base = src
        take = lambda e, shift=0: ref[base + e, pl.ds(at + shift, rows), :]
        centre = [take(e) for e in range(n)]
        below, above = z_neighbours(centre, self.number)
        out = []
        for e in range(n):
            c = lambda k: self.coef[k * n + e, pl.ds(at, rows), :]
            t = self.rhs[e, pl.ds(at, rows), :] - centre[e]
            t_x = c(0) * take(e, -self.pitch) + c(1) * take(e, self.pitch)
            t_y = c(2) * take(e, -1) + c(3) * take(e, 1)
            t_z = c(4) * below[e] + c(5) * above[e]
            out.append(t + (t_x + t_y) + t_z)
        return out, centre

    def sweep(self, pair, src, dst, first_x, count, first_y, rows, last=False, emit=None):
        def body(x):
            at = self.row(x, first_y)
            steps, centre = self.residual(src, at, rows)
            news = []
            for e in range(self.halves):
                new = pair[1] * steps[e]
                if pair[0] != 0.0:
                    new = pair[0] * self.update[e, pl.ds(at, rows), :] + new
                if not last:
                    self.update[e, pl.ds(at, rows), :] = new
                news.append(centre[e] + new)
            if emit is not None:
                emit(x, news)
            else:
                ref, base = dst
                for e in range(self.halves):
                    ref[base + e, pl.ds(at, rows), :] = news[e]

        plane_loop(first_x, count, body)

    def first_from_zero(self, pair, dst, first_x, count, first_y, rows):
        def body(x):
            at = self.row(x, first_y)
            for e in range(self.halves):
                new = pair[1] * self.rhs[e, pl.ds(at, rows), :]
                self.update[e, pl.ds(at, rows), :] = new
                ref, base = dst
                ref[base + e, pl.ds(at, rows), :] = new

        plane_loop(first_x, count, body)


def corner_pieces(sx, sy, depth):
    pieces = []
    for dx in range(1, depth):
        rows = depth - dx
        pieces.append((NX0 - dx if sx > 0 else dx - 1, NY0 - rows if sy > 0 else 0, rows))
    return pieces


def side_plane(sx, dx):
    return NX0 - dx if sx > 0 else dx - 1


def side_row(sy, dy):
    return NY0 - dy if sy > 0 else dy - 1


def corner_rows(depth):
    return depth * (depth - 1) // 2


def kernel(counts, *refs):
    inputs, out_hbm = refs[:6], refs[6]
    (nat, fine, fine_a, fine_b, coef0, diag0, rhs0, upd0, rest0,
     raw1, coef1, diag1, rhs1, upd1, it1_a, it1_b, rest1,
     raw2, coef2, diag2, rhs2, upd2, it2_a, it2_b,
     sxa, sya, sca, rxa, rya, rca, sxb, syb, scb, rxb, ryb, rcb,
     smc, rmc, rmcw, sg1, rg1, rg1w, sx1, rx1, rx1w,
     s2c, r2c, sg2, rg2, sxu, syu, scu, rxu, ryu, rcu, out_v,
     in_sem, out_sem, near_s, near_r, mids_s, mids_r, ball_s, ball_r) = refs[7:]
    count_x, count_y = counts
    me_x, me_y = lax.axis_index("gx"), lax.axis_index("gy")

    def device(offset):
        return (lax.rem(me_x + offset[0] + count_x, count_x), lax.rem(me_y + offset[1] + count_y, count_y))

    loads = [pltpu.make_async_copy(inputs[k], nat.at[k], in_sem.at[k]) for k in range(6)]
    for load in loads:
        load.start()
    barrier = pltpu.get_barrier_semaphore()
    for offset in BALL:
        pl.semaphore_signal(barrier, inc=1, device_id=device(offset), device_id_type=MESH)

    started = []

    def send(src, dst, s_sem, r_sem, offset):
        copy = pltpu.make_async_remote_copy(
            src_ref=src, dst_ref=dst, send_sem=s_sem, recv_sem=r_sem, device_id=device(offset), device_id_type=MESH
        )
        copy.start()
        started.append(copy)
        return copy

    level0 = Level(0, 2, row0, YP0, fine, coef0, diag0, rhs0, upd0)
    level1 = Level(1, 1, row1, YP1, raw1, coef1, diag1, rhs1, upd1)
    level2 = Level(2, 1, row2, YP2, raw2, coef2, diag2, rhs2, upd2)

    at = lanes((NY0, LANES))
    cell = 4 * (at % HALF) + 2 * (at // HALF)
    from_first = (at % HALF) < HALF // 2
    picks = [(cell + e) % LANES for e in range(2)]

    def permute(k):
        def body(x, carry):
            first = nat[k, x, :, 0:LANES]
            second = nat[k, x, :, LANES : 2 * LANES]
            for e in range(2):
                low = jnp.take_along_axis(first, picks[e], axis=1, mode="promise_in_bounds")
                high = jnp.take_along_axis(second, picks[e], axis=1, mode="promise_in_bounds")
                fine[2 * k + e, pl.ds(row0(x, 0), NY0), :] = jnp.where(from_first, low, high)
            return carry

        lax.fori_loop(0, NX0, body, 0)

    def pack(field, first, count, xs, ys, cs, planes, depth):
        def body(i, carry):
            k = first + i
            for side, (sx, _) in enumerate(NEAR[:2]):
                for dx in range(1, planes + 1):
                    dst = pl.multiple_of((i * planes + dx - 1) * NY0, NY0)
                    xs[side, pl.ds(dst, NY0), :] = field[k, pl.ds(row0(side_plane(sx, dx), 0), NY0), :]
            for side, (_, sy) in enumerate(NEAR[2:4]):
                for dy in range(1, depth + 1):
                    dst = pl.multiple_of((i * depth + dy - 1) * NX0, NX0)
                    ys[side, pl.ds(dst, NX0), :] = field[k, pl.ds(row0(0, side_row(sy, dy)), NX0, stride=YP0), :]
            for side, (sx, sy) in enumerate(NEAR[4:8]):
                dst = i * corner_rows(depth)
                for x, y, rows in corner_pieces(sx, sy, depth):
                    cs[side, pl.ds(dst, rows), :] = field[k, pl.ds(row0(x, y), rows), :]
                    dst = dst + rows
            return carry

        lax.fori_loop(0, count, body, 0)

    def unpack(field, first, count, xs, ys, cs, planes, depth):
        def body(i, carry):
            k = first + i
            for side, (sx, _) in enumerate(NEAR[:2]):
                for dx in range(1, planes + 1):
                    src = pl.multiple_of((i * planes + dx - 1) * NY0, NY0)
                    field[k, pl.ds(row0(side_plane(sx, dx) - sx * NX0, 0), NY0), :] = xs[side, pl.ds(src, NY0), :]
            for side, (_, sy) in enumerate(NEAR[2:4]):
                for dy in range(1, depth + 1):
                    src = pl.multiple_of((i * depth + dy - 1) * NX0, NX0)
                    to = pl.ds(row0(0, side_row(sy, dy) - sy * NY0), NX0, stride=YP0)
                    field[k, to, :] = ys[side, pl.ds(src, NX0), :]
            for side, (sx, sy) in enumerate(NEAR[4:8]):
                src = i * corner_rows(depth)
                for x, y, rows in corner_pieces(sx, sy, depth):
                    to = pl.ds(row0(x - sx * NX0, y - sy * NY0), rows)
                    field[k, to, :] = cs[side, pl.ds(src, rows), :]
                    src = src + rows
            return carry

        lax.fori_loop(0, count, body, 0)

    def extra_out(field, k, xs, base, sides):
        for side in sides:
            sx = NEAR[side][0]
            for e in range(2):
                xs[side, pl.ds(base + e * NY0, NY0), :] = field[k + e, pl.ds(row0(side_plane(sx, DEPTH), 0), NY0), :]

    def extra_in(field, k, xs, base, sides):
        for side in sides:
            sx = NEAR[side][0]
            for e in range(2):
                to = pl.ds(row0(side_plane(sx, DEPTH) - sx * NX0, 0), NY0)
                field[k + e, to, :] = xs[side, pl.ds(base + e * NY0, NY0), :]

    def near_sends(group, xs, ys, cs, rx, ry, rc, x_rows):
        waits = []
        for n, offset in enumerate(NEAR):
            s_sem, r_sem = near_s.at[group, n], near_r.at[group, n]
            if n < 2:
                cut = pl.ds(0, x_rows[n])
                waits.append(send(xs.at[n, cut], rx.at[n, cut], s_sem, r_sem, offset))
            elif n < 4:
                waits.append(send(ys.at[n - 2], ry.at[n - 2], s_sem, r_sem, offset))
            else:
                waits.append(send(cs.at[n - 4], rc.at[n - 4], s_sem, r_sem, offset))
        return waits

    for k in range(4):
        loads[k].wait()
        permute(k)
    pack(fine, 0, 8, sxa, sya, sca, 4, DEPTH)
    extra_out(fine, 2, sxa, 512, (0,))
    pl.semaphore_wait(barrier, len(BALL))
    waits_a = near_sends(0, sxa, sya, sca, rxa, rya, rca, (544, 512))
    for k in (4, 5):
        loads[k].wait()
        permute(k)
    pack(fine, 8, 4, sxb, syb, scb, 4, DEPTH)
    extra_out(fine, 10, sxb, 256, (0, 1))
    waits_b = near_sends(1, sxb, syb, scb, rxb, ryb, rcb, (288, 288))

    def children(k, e, x, y_step):
        return fine[2 * k + e, pl.ds(row0(x, y_step), NY1, stride=2), :]

    def coarsen1(big, carry):
        to = pl.ds(row1(big, 0), NY1)
        x = 2 * big
        absorb = sum(children(0, e, x + p, q) for e in range(2) for p in range(2) for q in range(2)) * 0.125
        face_x = sum(children(1, e, x, q) for e in range(2) for q in range(2)) * 0.25
        face_y = sum(children(2, e, x + p, 0) for e in range(2) for p in range(2)) * 0.25
        face_z = sum(children(3, 0, x + p, q) for p in range(2) for q in range(2)) * 0.25
        for k, value in enumerate((absorb, face_x, face_y, face_z)):
            raw1[k, to, :] = value
            smc[big, pl.ds(k * NY1, NY1), :] = value
        return carry

    lax.fori_loop(0, NX1, coarsen1, 0)

    def mid_sends(group, src, near, wide):
        waits = []
        for n, offset in enumerate(MIDS):
            s_sem, r_sem = mids_s.at[group, n], mids_r.at[group, n]
            if n < 8:
                waits.append(send(src, near.at[n], s_sem, r_sem, offset))
            else:
                cut = pl.ds(2 if offset[0] > 0 else 0, 2)
                waits.append(send(src.at[cut], wide.at[n - 8], s_sem, r_sem, offset))
        return waits

    waits_mc = mid_sends(0, smc, rmc, rmcw)

    def mid_unpack(near, wide, store):
        for n, (sx, sy) in enumerate(MIDS):
            planes = range(4) if n < 8 else (range(2, 4) if sx > 0 else range(2))
            for i, x in enumerate(planes):
                value = near[n, i] if n < 8 else wide[n - 8, i]
                store(row1(x - sx * NX1, -sy * NY1), value)

    def both(v):
        return v + pltpu.roll(v, HALF, 1)

    for big in range(NX2):
        grand = lambda k, x, q: raw1[k, pl.ds(row1(x, q), NY2, stride=2), :]
        x = 2 * big
        absorb = both(sum(grand(0, x + p, q) for p in range(2) for q in range(2))) * 0.125
        face_x = both(sum(grand(1, x, q) for q in range(2))) * 0.25
        face_y = both(sum(grand(2, x + p, 0) for p in range(2))) * 0.25
        face_z = sum(grand(3, x + p, q) for p in range(2) for q in range(2)) * 0.25
        low = lanes((NY2, LANES)) < HALF
        face_z = jnp.where(low, face_z, pltpu.roll(face_z, HALF, 1))
        for k, value in enumerate((absorb, face_x, face_y, face_z)):
            raw2[k, pl.ds(row2(big, 0), NY2), :] = value
        s2c[pl.ds(big * NY2, NY2), :] = jnp.where(low, absorb, face_x)
        s2c[pl.ds(8 + big * NY2, NY2), :] = jnp.where(low, face_y, face_z)

    for wait in waits_a:
        wait.wait_recv()
    unpack(fine, 0, 8, rxa, rya, rca, 4, DEPTH)
    extra_in(fine, 2, rxa, 512, (0,))
    for wait in waits_b:
        wait.wait_recv()
    unpack(fine, 8, 4, rxb, ryb, rcb, 4, DEPTH)
    extra_in(fine, 10, rxb, 256, (0, 1))
    level0.build(-4, 16, -4, 24, (fine, 8))
    weights = chebyshev_weights(SWEEPS)
    level0.sweep(weights[0], (fine, 10), (fine_a, 0), -4, 16, -4, 24)
    level0.sweep(weights[1], (fine_a, 0), (fine_b, 0), -3, 14, -4, 24)
    level0.sweep(weights[2], (fine_b, 0), (fine_a, 0), -2, 12, -4, 24)
    level0.sweep(weights[3], (fine_a, 0), (fine_b, 0), -1, 10, -4, 24, last=True)

    def rest_fine(x):
        at_row = row0(x, 0)
        steps, _ = level0.residual((fine_b, 0), at_row, NY0)
        for e in range(2):
            rest0[e, pl.ds(x * NY0, NY0), :] = steps[e] * diag0[e, pl.ds(at_row, NY0), :]

    plane_loop(0, NX0, rest_fine)

    face_x = sum(children(1, e, NX0, q) for e in range(2) for q in range(2)) * 0.25
    raw1[1, pl.ds(row1(NX1, 0), NY1), :] = face_x
    for wait in waits_mc:
        wait.wait_recv()

    def store_raw(to, value):
        for k in range(4):
            raw1[k, pl.ds(to, NY1), :] = value[k * NY1 : (k + 1) * NY1]

    mid_unpack(rmc, rmcw, store_raw)
    level1.build(-5, 14, -8, 24)
    for big in range(NX1):
        total = sum(
            rest0[e, pl.ds((2 * big + p) * NY0 + q, NY1, stride=2), :]
            for e in range(2) for p in range(2) for q in range(2)
        )
        value = total * 0.125 / diag1[0, pl.ds(row1(big, 0), NY1), :]
        rhs1[0, pl.ds(row1(big, 0), NY1), :] = value
        sg1[big] = value

    waits_g1 = mid_sends(1, sg1, rg1, rg1w)
    waits_2c = [send(s2c, r2c.at[n], ball_s.at[0, n], ball_r.at[0, n], o) for n, o in enumerate(BALL)]

    x = NX1
    grand = lambda k, x, y: raw1[k, pl.ds(row1(x, y), NY2, stride=2), :]
    raw2[1, pl.ds(row2(NX2, 0), NY2), :] = both(grand(1, x, 0) + grand(1, x, 1)) * 0.25
    for big in range(NX2):
        above = both(sum(grand(2, 2 * big + p, NY1) for p in range(2))) * 0.25
        raw2[2, pl.ds(row2(big, NY2), 1), :] = above[0:1]
    diag_own2 = [level2.own_diagonal(big, 0, NY2)[0] for big in range(NX2)]

    def store_rhs1(to, value):
        rhs1[0, pl.ds(to, NY1), :] = value

    for wait in waits_g1:
        wait.wait_recv()
    mid_unpack(rg1, rg1w, store_rhs1)
    level1.first_from_zero(weights[0], (it1_a, 0), -4, 12, -4, 16)
    level1.sweep(weights[1], (it1_a, 0), (it1_b, 0), -3, 10, -4, 16)
    level1.sweep(weights[2], (it1_b, 0), (it1_a, 0), -2, 8, -4, 16)
    level1.sweep(weights[3], (it1_a, 0), (it1_b, 0), -1, 6, -4, 16, last=True)

    def rest_mid(x):
        at_row = row1(x, 0)
        steps, centre = level1.residual((it1_b, 0), at_row, NY1)
        rest1[pl.ds(x * NY1, NY1), :] = steps[0] * diag1[0, pl.ds(at_row, NY1), :]
        sx1[x] = centre[0]

    plane_loop(0, NX1, rest_mid)
    for big in range(NX2):
        total = sum(rest1[pl.ds((2 * big + p) * NY1 + q, NY2, stride=2), :] for p in range(2) for q in range(2))
        value = both(total) * 0.125 / diag_own2[big]
        rhs2[0, pl.ds(row2(big, 0), NY2), :] = value
        sg2[pl.ds(big * NY2, NY2), :] = value

    waits_g2 = [send(sg2, rg2.at[n], ball_s.at[1, n], ball_r.at[1, n], o) for n, o in enumerate(BALL)]
    waits_x1 = mid_sends(2, sx1, rx1, rx1w)
    pack(fine_b, 0, 2, sxu, syu, scu, 4, 4)
    waits_x0 = near_sends(2, sxu, syu, scu, rxu, ryu, rcu, (128, 128))

    for wait in waits_2c:
        wait.wait_recv()
    low8 = lanes((8, LANES)) < HALF
    for n, (i, j) in enumerate(BALL):
        for part in range(2):
            value = r2c[n, pl.ds(8 * part, 8), :]
            other = pltpu.roll(value, HALF, 1)
            for k, full in enumerate((jnp.where(low8, value, other), jnp.where(low8, other, value))):
                for p in range(NX2):
                    to = pl.ds(row2(p - 2 * i, -4 * j), NY2)
                    raw2[2 * part + k, to, :] = full[p * NY2 : (p + 1) * NY2]
    level2.build(-9, 20, -10, 24)
    for wait in waits_g2:
        wait.wait_recv()
    for n, (i, j) in enumerate(BALL):
        for p in range(NX2):
            rhs2[0, pl.ds(row2(p - 2 * i, -4 * j), NY2), :] = rg2[n, pl.ds(p * NY2, NY2), :]
    coarse = chebyshev_weights(COARSE_SWEEPS)
    level2.first_from_zero(coarse[0], (it2_a, 0), -10, 22, -10, 24)
    src, dst = it2_a, it2_b
    for sweep in range(1, COARSE_SWEEPS):
        reach = COARSE_SWEEPS - 1 - sweep
        first_y, rows = (-10, 24) if reach > 3 else (-6, 16)
        level2.sweep(coarse[sweep], (src, 0), (dst, 0), -3 - reach, 8 + 2 * reach, first_y, rows, last=reach == 0)
        src, dst = dst, src

    def store_it1(to, value):
        it1_b[0, pl.ds(to, NY1), :] = value

    for wait in waits_x1:
        wait.wait_recv()
    mid_unpack(rx1, rx1w, store_it1)

    def lift1(big):
        for y in (-3, -1):
            value = src[0, pl.ds(row2(big, y), 8), :]
            for p in range(2):
                for q in range(2):
                    to = pl.ds(row1(2 * big + p, 2 * y + q), 8, stride=2)
                    it1_a[0, to, :] = it1_b[0, to, :] + value

    plane_loop(-3, 8, lift1)
    level1.sweep(weights[0], (it1_a, 0), (it1_b, 0), -5, 14, -8, 24)
    level1.sweep(weights[1], (it1_b, 0), (it1_a, 0), -4, 12, -8, 24)
    level1.sweep(weights[2], (it1_a, 0), (it1_b, 0), -3, 10, -4, 16)
    level1.sweep(weights[3], (it1_b, 0), (it1_a, 0), -2, 8, -4, 16, last=True)

    for wait in waits_x0:
        wait.wait_recv()
    unpack(fine_b, 0, 2, rxu, ryu, rcu, 4, 4)

    def lift0(big):
        for y in (-2, 2):
            value = it1_a[0, pl.ds(row1(big, y), 8), :]
            for e in range(2):
                for p in range(2):
                    for q in range(2):
                        to = pl.ds(row0(2 * big + p, 2 * y + q), 8, stride=2)
                        fine_a[e, to, :] = fine_b[e, to, :] + value

    plane_loop(-2, 8, lift0)
    level0.sweep(weights[0], (fine_a, 0), (fine_b, 0), -3, 14, -4, 24)
    level0.sweep(weights[1], (fine_b, 0), (fine_a, 0), -2, 12, -4, 24)
    level0.sweep(weights[2], (fine_a, 0), (fine_b, 0), -1, 10, -4, 24)
    back = HALF * ((at // 2) % 2) + at // 4
    even = (at % 2) == 0

    def emit(x, news):
        for half in range(2):
            pick = back + 32 * half
            lower = jnp.take_along_axis(news[0], pick, axis=1, mode="promise_in_bounds")
            upper = jnp.take_along_axis(news[1], pick, axis=1, mode="promise_in_bounds")
            out_v[x, :, half * LANES : (half + 1) * LANES] = jnp.where(even, lower, upper)

    level0.sweep(weights[3], (fine_b, 0), None, 0, 8, 0, NY0, last=True, emit=emit)
    store = pltpu.make_async_copy(out_v, out_hbm, out_sem.at[0])
    store.start()
    for copy in started:
        copy.wait_send()
    store.wait()


def solution(mesh):
    counts = (mesh.shape["gx"], mesh.shape["gy"])

    def local(source, initial, absorption, beta_x, beta_y, beta_z):
        f32 = jnp.float32
        v = lambda *shape: pltpu.VMEM(shape, f32)
        scratch = [
            v(6, NX0, NY0, 256), v(12, ROWS0, LANES), v(2, ROWS0, LANES), v(2, ROWS0, LANES),
            v(12, ROWS0, LANES), v(2, ROWS0, LANES), v(2, ROWS0, LANES), v(2, ROWS0, LANES), v(2, 128, LANES),
            v(4, ROWS1, LANES), v(6, ROWS1, LANES), v(1, ROWS1, LANES), v(1, ROWS1, LANES), v(1, ROWS1, LANES),
            v(1, ROWS1, LANES), v(1, ROWS1, LANES), v(32, LANES),
            v(4, ROWS2, LANES), v(6, ROWS2, LANES), v(1, ROWS2, LANES), v(1, ROWS2, LANES), v(1, ROWS2, LANES),
            v(1, ROWS2, LANES), v(1, ROWS2, LANES),
            v(2, 544, LANES), v(2, 320, LANES), v(4, 80, LANES),
            v(2, 544, LANES), v(2, 320, LANES), v(4, 80, LANES),
            v(2, 288, LANES), v(2, 160, LANES), v(4, 40, LANES),
            v(2, 288, LANES), v(2, 160, LANES), v(4, 40, LANES),
            v(4, 32, LANES), v(8, 4, 32, LANES), v(6, 2, 32, LANES),
            v(4, 8, LANES), v(8, 4, 8, LANES), v(6, 2, 8, LANES),
            v(4, 8, LANES), v(8, 4, 8, LANES), v(6, 2, 8, LANES),
            v(16, LANES), v(len(BALL), 16, LANES), v(8, LANES), v(len(BALL), 8, LANES),
            v(2, 128, LANES), v(2, 64, LANES), v(4, 16, LANES),
            v(2, 128, LANES), v(2, 64, LANES), v(4, 16, LANES),
            v(NX0, NY0, 256),
            pltpu.SemaphoreType.DMA((6,)), pltpu.SemaphoreType.DMA((1,)),
            pltpu.SemaphoreType.DMA((3, 8)), pltpu.SemaphoreType.DMA((3, 8)),
            pltpu.SemaphoreType.DMA((3, len(MIDS))), pltpu.SemaphoreType.DMA((3, len(MIDS))),
            pltpu.SemaphoreType.DMA((2, len(BALL))), pltpu.SemaphoreType.DMA((2, len(BALL))),
        ]
        call = pl.pallas_call(
            lambda *refs: kernel(counts, *refs),
            out_shape=jax.ShapeDtypeStruct((NX0, NY0, 256), f32),
            in_specs=[pl.BlockSpec(memory_space=pl.ANY)] * 6,
            out_specs=pl.BlockSpec(memory_space=pl.ANY),
            scratch_shapes=scratch,
            compiler_params=pltpu.CompilerParams(
                collective_id=0, has_side_effects=True, vmem_limit_bytes=56 * 2**20
            ),
            name="vcycle",
        )
        return call(absorption, beta_x, beta_y, beta_z, source, initial)

    return jax.shard_map(
        local,
        mesh=mesh,
        in_specs=(P("gx", "gy", None),) * 6,
        out_specs=P("gx", "gy", None),
        check_vma=False,
    )
```

time: 436 us -> 71.4 us (0.16)
  starting transfers between devices: 334 us -> 0 us
  Pallas kernels: 0 us -> 69.7 us
  local copies, waits for them, and re-layouts: 48.6 us -> 1.57 us
  waiting for transfers between devices: 30.3 us -> 0 us
  other arithmetic: 18.1 us -> 0 us
    ppermute x98 -> x0, starting transfers between devices: 334 us -> none  [the longest x48 275 us: extended(): lax.ppermute(lax.slice_in_dim(block, 0, width, axis=dim), axis, backward)]
    pallas_call x0 -> x1, Pallas kernels: none -> 69.7 us  [local(): return call(absorption, beta_x, beta_y, beta_z, source, initial)]
    ppermute x98 -> x0, waiting for transfers between devices: 30.3 us -> none  [the longest x48 17.4 us: extended(): lax.ppermute(lax.slice_in_dim(block, 0, width, axis=dim), axis, backward)]
    reshape x8 -> x0, local copies, waits for them, and re-layouts: 29.9 us -> none  [the longest x3 20.6 us: restrict_cells(): field.reshape(size_x // 2, 2, size_y // 2, 2, size_z // 2, 2)]
    reduce_sum x14 -> x0, other arithmetic: 13.1 us -> none  [the longest x4 8.43 us: restrict_cells(): field.reshape(size_x // 2, 2, size_y // 2, 2, size_z // 2, 2)]
    slice x69 -> x0, local copies, waits for them, and re-layouts: 11.7 us -> none  [the longest x24 2.86 us: apply_operator(): lower_z = jnp.concatenate([zeros_plane, field[:, :, :-1]], axis=2)]
    add x24 -> x0, other arithmetic: 4.37 us -> none  [the longest x22 4.35 us: chebyshev_smooth(): iterate = iterate + update]
  transfers between devices with their start and end apart: 98 -> 0, of which waited for: 66 -> 0; matrix products, arithmetic and copies ran while one was open for 8% -> 0% of each run, Pallas kernels for 0% -> 0%
where the time goes in v1:
time: 71.4 us; the launch traced here: 71.3 us
  Pallas kernels  69.7 us (98%)
  local copies, waits for them, and re-layouts  1.57 us (2%)
    pallas_call x1, Pallas kernels, local(): return call(absorption, beta_x, beta_y, beta_z, source, initial)  69.7 us
    unnamed x1, local copies, waits for them, and re-layouts  1.57 us

profile of v1, /device:TPU:1, one launch (start us, length us, event | category | flops | bytes accessed | tf_op | source)
XLA Modules:
  0.0 71.3 jit_solution(6114101034768629354)
XLA Ops:
  0.0 69.7 %vcycle.1 = f32[8,16,256]{2,1,0:T(8,128)} custom-call(f32[8,16,256]{2,1,0:T(8,128)} %refs_0_.1, f32[8,16,256]{2,1,0:T(8,128)} %refs_1_.1, f32[8,16,256]{2,1,0:T(8,128)} %refs_2_.1, f32[8,16,256]{2,1,0:T(8,128)} %refs_3_.1, f32[8,16,256]{2,1,0:T(8,128)} %refs_4_.1, f32[8,16,256]{2,1,0:T(8,128)} %refs_5_.1), custom_call_target="tpu_custom_call" | custom-call | tf_op jit(solution)/shard_map/vcycle/pallas_call | solution.py:610
  69.7 1.6 %copy.8 = f32[8,16,256]{2,1,0:T(8,128)} copy(f32[8,16,256]{2,1,0:T(8,128)} %vcycle.1) | data formatting | bytes 262144

commit v2 on v1

v2 whole, which is shorter than its diff:
```python
import jax
import jax.numpy as jnp
from jax import lax
from jax.experimental import pallas as pl
from jax.experimental.pallas import tpu as pltpu
from jax.sharding import PartitionSpec as P

SWEEPS = 4
COARSE_SWEEPS = 8
LANES = 128
HALF = 64
GROUP = 4
MESH = pl.DeviceIdType.MESH

NX0, NY0, HX0, HY0, YP0 = 8, 16, 5, 5, 26
NX1, NY1, HX1, HY1, YP1 = 4, 8, 6, 9, 26
NX2, NY2, HX2, HY2, YP2 = 2, 4, 10, 12, 28
ROWS0 = 472
ROWS1 = 416
ROWS2 = 616

DEPTH = 5
NEAR = [(-1, 0), (1, 0), (0, -1), (0, 1), (-1, -1), (-1, 1), (1, -1), (1, 1)]
WIDE = [(-2, 0), (2, 0), (-2, -1), (-2, 1), (2, -1), (2, 1)]
MIDS = NEAR + WIDE


def ball_offsets():
    offsets = []
    for i in range(-5, 6):
        for j in range(-3, 4):
            far_x = 2 * abs(i) - 1 if i else 0
            far_y = 4 * abs(j) - 3 if j else 0
            if (i, j) != (0, 0) and far_x + far_y <= (11 if i and j else 10):
                offsets.append((i, j))
    return offsets


BALL = ball_offsets()


def chebyshev_weights(sweeps):
    cheb_theta = 1.125
    cheb_delta = 0.875
    cheb_sigma = cheb_theta / cheb_delta
    rho_old = 1.0 / cheb_sigma
    weights = [(0.0, 1.0 / cheb_theta)]
    for sweep in range(1, sweeps):
        rho_new = 1.0 / (2.0 * cheb_sigma - rho_old)
        weights.append((rho_new * rho_old, 2.0 * rho_new / cheb_delta))
        rho_old = rho_new
    return weights


def row0(x, y):
    return (x + HX0) * YP0 + y + HY0


def row1(x, y):
    return (x + HX1) * YP1 + y + HY1


def row2(x, y):
    return (x + HX2) * YP2 + y + HY2


def lanes(shape):
    return lax.broadcasted_iota(jnp.int32, shape, len(shape) - 1)


def shift_down(v):
    return jnp.where(lanes(v.shape) < HALF, pltpu.roll(v, HALF + 1, 1), pltpu.roll(v, HALF, 1))


def shift_up(v):
    return jnp.where(lanes(v.shape) < HALF, pltpu.roll(v, HALF, 1), pltpu.roll(v, HALF - 1, 1))


def z_neighbours(values, level):
    if level == 0:
        return (shift_down(values[1]), values[0]), (values[1], shift_up(values[0]))
    if level == 1:
        return (shift_down(values[0]),), (shift_up(values[0]),)
    return (pltpu.roll(values[0], 1, 1),), (pltpu.roll(values[0], LANES - 1, 1),)


def z_ends(shape, level, half):
    at = lanes(shape)
    if level == 0:
        return (at == 0) if half == 0 else None, (at == LANES - 1) if half == 1 else None
    if level == 1:
        return at == 0, at == LANES - 1
    return (at % HALF) == 0, (at % HALF) == HALF - 1


def plane_loop(first, count, body, group=GROUP):
    def several(start, n):
        stores = []
        for i in range(n):
            stores += body(start + i)
        for ref, index, value in stores:
            ref[index] = value

    def step(i, carry):
        several(first + group * i, group)
        return carry

    if count // group > 1:
        lax.fori_loop(0, count // group, step, 0)
        done = count // group * group
    else:
        done = 0
    if done < count:
        several(first + done, count - done)


class Level:
    def __init__(self, number, halves, row, pitch, raw, coef, diag, rhs, update):
        self.number, self.halves, self.row, self.pitch = number, halves, row, pitch
        self.raw, self.coef, self.diag, self.rhs, self.update = raw, coef, diag, rhs, update
        self.scale = 0.25**number

    def faces(self, at, rows):
        n, raw = self.halves, self.raw
        take = lambda k, e, shift=0: raw[k * n + e, pl.ds(at + shift, rows), :]
        low_z = [take(3, e) for e in range(n)]
        _, high_z = z_neighbours(low_z, self.number)
        out = []
        for e in range(n):
            _, top = z_ends((rows, LANES), self.number, e)
            upper = high_z[e] if top is None else jnp.where(top, 0.0, high_z[e])
            faces = [take(1, e), take(1, e, self.pitch), take(2, e), take(2, e, 1), low_z[e], upper]
            total = (faces[0] + faces[1]) + (faces[2] + faces[3]) + (faces[4] + faces[5])
            out.append((faces, take(0, e) + self.scale * total))
        return out

    def own_diagonal(self, x, y, rows):
        return [d for _, d in self.faces(self.row(x, y), rows)]

    def build(self, first_x, count, first_y, rows, source=None):
        n = self.halves

        def body(x):
            at = self.row(x, first_y)
            stores = []
            for e, (faces, diagonal) in enumerate(self.faces(at, rows)):
                inverse = 1.0 / diagonal
                low, _ = z_ends((rows, LANES), self.number, e)
                if low is not None:
                    faces[4] = jnp.where(low, 0.0, faces[4])
                scaled = self.scale * inverse
                for c in range(6):
                    stores.append((self.coef, (c * n + e, pl.ds(at, rows)), faces[c] * scaled))
                stores.append((self.diag, (e, pl.ds(at, rows)), diagonal))
                if source is not None:
                    ref, base = source
                    stores.append((self.rhs, (e, pl.ds(at, rows)), ref[base + e, pl.ds(at, rows), :] * inverse))
            return stores

        plane_loop(first_x, count, body)

    def residual(self, src, at, rows):
        n = self.halves
        ref, base = src
        take = lambda e, shift=0: ref[base + e, pl.ds(at + shift, rows), :]
        centre = [take(e) for e in range(n)]
        below, above = z_neighbours(centre, self.number)
        out = []
        for e in range(n):
            c = lambda k: self.coef[k * n + e, pl.ds(at, rows), :]
            t = self.rhs[e, pl.ds(at, rows), :] - centre[e]
            t_x = c(0) * take(e, -self.pitch) + c(1) * take(e, self.pitch)
            t_y = c(2) * take(e, -1) + c(3) * take(e, 1)
            t_z = c(4) * below[e] + c(5) * above[e]
            out.append(t + (t_x + t_y) + t_z)
        return out, centre

    def sweep(self, pair, src, dst, first_x, count, first_y, rows, last=False, emit=None):
        def body(x):
            at = self.row(x, first_y)
            steps, centre = self.residual(src, at, rows)
            news, stores = [], []
            for e in range(self.halves):
                new = pair[1] * steps[e]
                if pair[0] != 0.0:
                    new = pair[0] * self.update[e, pl.ds(at, rows), :] + new
                if not last:
                    stores.append((self.update, (e, pl.ds(at, rows)), new))
                news.append(centre[e] + new)
            if emit is not None:
                return emit(x, news)
            ref, base = dst
            return stores + [(ref, (base + e, pl.ds(at, rows)), news[e]) for e in range(self.halves)]

        plane_loop(first_x, count, body)

    def first_from_zero(self, pair, dst, first_x, count, first_y, rows):
        def body(x):
            at = self.row(x, first_y)
            ref, base = dst
            stores = []
            for e in range(self.halves):
                new = pair[1] * self.rhs[e, pl.ds(at, rows), :]
                stores.append((self.update, (e, pl.ds(at, rows)), new))
                stores.append((ref, (base + e, pl.ds(at, rows)), new))
            return stores

        plane_loop(first_x, count, body)


def corner_pieces(sx, sy, depth):
    pieces = []
    for dx in range(1, depth):
        rows = depth - dx
        pieces.append((NX0 - dx if sx > 0 else dx - 1, NY0 - rows if sy > 0 else 0, rows))
    return pieces


def side_plane(sx, dx):
    return NX0 - dx if sx > 0 else dx - 1


def side_row(sy, dy):
    return NY0 - dy if sy > 0 else dy - 1


def near_plan(fields, planes, depth, extra=(0, 0)):
    sizes = [fields * planes * NY0 + extra[0], fields * planes * NY0 + extra[1]]
    sizes += [fields * depth * NX0] * 2 + [-(-fields * corner_rows(depth) // 8) * 8] * 4
    starts = [sum(sizes[:n]) for n in range(8)]
    return list(zip(starts, sizes)), sum(sizes)


def corner_rows(depth):
    return depth * (depth - 1) // 2


RAW_A, RAW_B, MID_COEF, LOW_COEF, MID_RHS, LOW_RHS, MID_ITER, FINE_ITER = range(8)
PLAN_A, SIZE_A = near_plan(8, 4, DEPTH, (32, 0))
PLAN_B, SIZE_B = near_plan(4, 4, DEPTH, (32, 32))
PLAN_U, SIZE_U = near_plan(2, 4, 4)


def kernel(counts, *refs):
    inputs, out_hbm = refs[:6], refs[6]
    (nat, fine, fine_a, fine_b, coef0, diag0, rhs0, upd0, rest0,
     raw1, coef1, diag1, rhs1, upd1, it1_a, it1_b, rest1,
     raw2, coef2, diag2, rhs2, upd2, it2_a, it2_b,
     sra, rra, srb, rrb, smc, rmc, sg1, rg1, sx1, rx1, s2c, r2c, sg2, rg2, siu, riu, out_v,
     in_sem, out_sem, sent, got) = refs[7:]
    count_x, count_y = counts
    me_x, me_y = lax.axis_index("gx"), lax.axis_index("gy")

    def device(offset):
        return (lax.rem(me_x + offset[0] + count_x, count_x), lax.rem(me_y + offset[1] + count_y, count_y))

    loads = [pltpu.make_async_copy(inputs[k], nat.at[k], in_sem.at[k]) for k in range(6)]
    for load in loads:
        load.start()
    barrier = pltpu.get_barrier_semaphore()
    for offset in NEAR + [o for o in BALL if o not in NEAR]:
        pl.semaphore_signal(barrier, inc=1, device_id=device(offset), device_id_type=MESH)

    def send(group, src, dst, offset):
        pltpu.make_async_remote_copy(
            src_ref=src, dst_ref=dst, send_sem=sent.at[group], recv_sem=got.at[group],
            device_id=device(offset), device_id_type=MESH,
        ).start()

    def arrived(group, landing):
        pltpu.make_async_copy(landing, landing, got.at[group]).wait()

    def departed(group, landing):
        pltpu.make_async_copy(landing, landing, sent.at[group]).wait()

    level0 = Level(0, 2, row0, YP0, fine, coef0, diag0, rhs0, upd0)
    level1 = Level(1, 1, row1, YP1, raw1, coef1, diag1, rhs1, upd1)
    level2 = Level(2, 1, row2, YP2, raw2, coef2, diag2, rhs2, upd2)

    at = lanes((NY0, LANES))
    cell = 4 * (at % HALF) + 2 * (at // HALF)
    from_first = (at % HALF) < HALF // 2
    picks = [(cell + e) % LANES for e in range(2)]

    def permute(k):
        def body(x):
            first = nat[k, x, :, 0:LANES]
            second = nat[k, x, :, LANES : 2 * LANES]
            stores = []
            for e in range(2):
                low = jnp.take_along_axis(first, picks[e], axis=1, mode="promise_in_bounds")
                high = jnp.take_along_axis(second, picks[e], axis=1, mode="promise_in_bounds")
                stores.append((fine, (2 * k + e, pl.ds(row0(x, 0), NY0)), jnp.where(from_first, low, high)))
            return stores

        plane_loop(0, NX0, body)

    def near_rows(i, plan, planes, depth):
        for n, (sx, sy) in enumerate(NEAR):
            shift = -(sx * NX0 * YP0 + sy * NY0)
            start = plan[n][0]
            if n < 2:
                for dx in range(1, planes + 1):
                    at_buffer = pl.multiple_of(start + (i * planes + dx - 1) * NY0, 8)
                    yield row0(side_plane(sx, dx), 0), NY0, None, shift, at_buffer
            elif n < 4:
                for dy in range(1, depth + 1):
                    at_buffer = pl.multiple_of(start + (i * depth + dy - 1) * NX0, 8)
                    yield row0(0, side_row(sy, dy)), NX0, YP0, shift, at_buffer
            else:
                at_buffer = start + i * corner_rows(depth)
                for x, y, rows in corner_pieces(sx, sy, depth):
                    yield row0(x, y), rows, None, shift, at_buffer
                    at_buffer = at_buffer + rows

    def pack(field, first, count, out, plan, planes, depth):
        def body(i, carry):
            values = []
            for row, rows, stride, _, to in near_rows(i, plan, planes, depth):
                values.append((to, rows, field[first + i, pl.ds(row, rows, stride=stride), :]))
            for to, rows, value in values:
                out[pl.ds(to, rows), :] = value
            return carry

        lax.fori_loop(0, count, body, 0)

    def unpack(field, first, count, landing, plan, planes, depth):
        def body(i, carry):
            values = []
            for row, rows, stride, shift, at_buffer in near_rows(i, plan, planes, depth):
                values.append((pl.ds(row + shift, rows, stride=stride), landing[pl.ds(at_buffer, rows), :]))
            for to, value in values:
                field[first + i, to, :] = value
            return carry

        lax.fori_loop(0, count, body, 0)

    def extra_pieces(k, plan, base, sides):
        for side in sides:
            sx = NEAR[side][0]
            for e in range(2):
                row = row0(side_plane(sx, DEPTH), 0)
                yield k + e, row, row - sx * NX0 * YP0, plan[side][0] + base + e * NY0

    def extra_out(field, k, out, plan, base, sides):
        for f, row, _, to in extra_pieces(k, plan, base, sides):
            out[pl.ds(to, NY0), :] = field[f, pl.ds(row, NY0), :]

    def extra_in(field, k, landing, plan, base, sides):
        for f, _, row, at_buffer in extra_pieces(k, plan, base, sides):
            field[f, pl.ds(row, NY0), :] = landing[pl.ds(at_buffer, NY0), :]

    def near_sends(group, out, landing, plan):
        for (start, rows), offset in zip(plan, NEAR):
            cut = pl.ds(start, rows)
            send(group, out.at[cut], landing.at[cut], offset)

    for k in range(4):
        loads[k].wait()
        permute(k)
    pack(fine, 0, 8, sra, PLAN_A, 4, DEPTH)
    extra_out(fine, 2, sra, PLAN_A, 512, (0,))
    pl.semaphore_wait(barrier, len(BALL))
    near_sends(RAW_A, sra, rra, PLAN_A)
    for k in (4, 5):
        loads[k].wait()
        permute(k)
    pack(fine, 8, 4, srb, PLAN_B, 4, DEPTH)
    extra_out(fine, 10, srb, PLAN_B, 256, (0, 1))
    near_sends(RAW_B, srb, rrb, PLAN_B)

    def children(k, e, x, y_step):
        return fine[2 * k + e, pl.ds(row0(x, y_step), NY1, stride=2), :]

    def coarsen1(big):
        to = pl.ds(row1(big, 0), NY1)
        x = 2 * big
        absorb = sum(children(0, e, x + p, q) for e in range(2) for p in range(2) for q in range(2)) * 0.125
        face_x = sum(children(1, e, x, q) for e in range(2) for q in range(2)) * 0.25
        face_y = sum(children(2, e, x + p, 0) for e in range(2) for p in range(2)) * 0.25
        face_z = sum(children(3, 0, x + p, q) for p in range(2) for q in range(2)) * 0.25
        for k, value in enumerate((absorb, face_x, face_y, face_z)):
            raw1[k, to, :] = value
            smc[big, pl.ds(k * NY1, NY1), :] = value

    for big in range(NX1):
        coarsen1(big)

    def mid_sends(group, src, landing):
        for n, offset in enumerate(MIDS):
            if n < 8:
                send(group, src, landing.at[pl.ds(4 * n, 4)], offset)
            else:
                cut = pl.ds(2 if offset[0] > 0 else 0, 2)
                send(group, src.at[cut], landing.at[pl.ds(16 + 2 * n, 2)], offset)

    mid_sends(MID_COEF, smc, rmc)

    def mid_unpack(landing, store):
        for n, (sx, sy) in enumerate(MIDS):
            planes = range(4) if n < 8 else (range(2, 4) if sx > 0 else range(2))
            first = 4 * n if n < 8 else 16 + 2 * n
            for i, x in enumerate(planes):
                store(row1(x - sx * NX1, -sy * NY1), landing[first + i])

    def both(v):
        return v + pltpu.roll(v, HALF, 1)

    for big in range(NX2):
        grand = lambda k, x, q: raw1[k, pl.ds(row1(x, q), NY2, stride=2), :]
        x = 2 * big
        absorb = both(sum(grand(0, x + p, q) for p in range(2) for q in range(2))) * 0.125
        face_x = both(sum(grand(1, x, q) for q in range(2))) * 0.25
        face_y = both(sum(grand(2, x + p, 0) for p in range(2))) * 0.25
        face_z = sum(grand(3, x + p, q) for p in range(2) for q in range(2)) * 0.25
        low = lanes((NY2, LANES)) < HALF
        face_z = jnp.where(low, face_z, pltpu.roll(face_z, HALF, 1))
        for k, value in enumerate((absorb, face_x, face_y, face_z)):
            raw2[k, pl.ds(row2(big, 0), NY2), :] = value
        s2c[pl.ds(big * NY2, NY2), :] = jnp.where(low, absorb, face_x)
        s2c[pl.ds(8 + big * NY2, NY2), :] = jnp.where(low, face_y, face_z)

    def ball_sends(group, src, landing):
        for n, offset in enumerate(BALL):
            send(group, src, landing.at[n], offset)

    ball_sends(LOW_COEF, s2c, r2c)

    arrived(RAW_A, rra)
    unpack(fine, 0, 8, rra, PLAN_A, 4, DEPTH)
    extra_in(fine, 2, rra, PLAN_A, 512, (0,))
    arrived(RAW_B, rrb)
    unpack(fine, 8, 4, rrb, PLAN_B, 4, DEPTH)
    extra_in(fine, 10, rrb, PLAN_B, 256, (0, 1))
    level0.build(-4, 16, -4, 24, (fine, 8))
    weights = chebyshev_weights(SWEEPS)
    level0.sweep(weights[0], (fine, 10), (fine_a, 0), -4, 16, -4, 24)
    level0.sweep(weights[1], (fine_a, 0), (fine_b, 0), -3, 14, -4, 24)
    level0.sweep(weights[2], (fine_b, 0), (fine_a, 0), -2, 12, -4, 24)
    level0.sweep(weights[3], (fine_a, 0), (fine_b, 0), -1, 10, -4, 24, last=True)

    def rest_fine(x):
        at_row = row0(x, 0)
        steps, _ = level0.residual((fine_b, 0), at_row, NY0)
        return [
            (rest0, (e, pl.ds(x * NY0, NY0)), steps[e] * diag0[e, pl.ds(at_row, NY0), :]) for e in range(2)
        ]

    plane_loop(0, NX0, rest_fine)

    face_x = sum(children(1, e, NX0, q) for e in range(2) for q in range(2)) * 0.25
    raw1[1, pl.ds(row1(NX1, 0), NY1), :] = face_x
    arrived(MID_COEF, rmc)

    def store_raw(to, value):
        for k in range(4):
            raw1[k, pl.ds(to, NY1), :] = value[k * NY1 : (k + 1) * NY1]

    mid_unpack(rmc, store_raw)
    level1.build(-5, 14, -8, 24)
    for big in range(NX1):
        total = sum(
            rest0[e, pl.ds((2 * big + p) * NY0 + q, NY1, stride=2), :]
            for e in range(2) for p in range(2) for q in range(2)
        )
        value = total * 0.125 / diag1[0, pl.ds(row1(big, 0), NY1), :]
        rhs1[0, pl.ds(row1(big, 0), NY1), :] = value
        sg1[big] = value

    mid_sends(MID_RHS, sg1, rg1)

    x = NX1
    grand = lambda k, x, y: raw1[k, pl.ds(row1(x, y), NY2, stride=2), :]
    raw2[1, pl.ds(row2(NX2, 0), NY2), :] = both(grand(1, x, 0) + grand(1, x, 1)) * 0.25
    for big in range(NX2):
        above = both(sum(grand(2, 2 * big + p, NY1) for p in range(2))) * 0.25
        raw2[2, pl.ds(row2(big, NY2), 1), :] = above[0:1]
    diag_own2 = [level2.own_diagonal(big, 0, NY2)[0] for big in range(NX2)]

    def store_rhs1(to, value):
        rhs1[0, pl.ds(to, NY1), :] = value

    arrived(MID_RHS, rg1)
    mid_unpack(rg1, store_rhs1)
    level1.first_from_zero(weights[0], (it1_a, 0), -4, 12, -4, 16)
    level1.sweep(weights[1], (it1_a, 0), (it1_b, 0), -3, 10, -4, 16)
    level1.sweep(weights[2], (it1_b, 0), (it1_a, 0), -2, 8, -4, 16)
    level1.sweep(weights[3], (it1_a, 0), (it1_b, 0), -1, 6, -4, 16, last=True)

    def rest_mid(x):
        at_row = row1(x, 0)
        steps, centre = level1.residual((it1_b, 0), at_row, NY1)
        return [
            (rest1, (pl.ds(x * NY1, NY1),), steps[0] * diag1[0, pl.ds(at_row, NY1), :]),
            (sx1, (x,), centre[0]),
        ]

    plane_loop(0, NX1, rest_mid)
    for big in range(NX2):
        total = sum(rest1[pl.ds((2 * big + p) * NY1 + q, NY2, stride=2), :] for p in range(2) for q in range(2))
        value = both(total) * 0.125 / diag_own2[big]
        rhs2[0, pl.ds(row2(big, 0), NY2), :] = value
        sg2[pl.ds(big * NY2, NY2), :] = value

    ball_sends(LOW_RHS, sg2, rg2)
    mid_sends(MID_ITER, sx1, rx1)
    pack(fine_b, 0, 2, siu, PLAN_U, 4, 4)
    near_sends(FINE_ITER, siu, riu, PLAN_U)

    arrived(LOW_COEF, r2c)
    low8 = lanes((8, LANES)) < HALF
    for n, (i, j) in enumerate(BALL):
        for part in range(2):
            value = r2c[n, pl.ds(8 * part, 8), :]
            other = pltpu.roll(value, HALF, 1)
            for k, full in enumerate((jnp.where(low8, value, other), jnp.where(low8, other, value))):
                for p in range(NX2):
                    to = pl.ds(row2(p - 2 * i, -4 * j), NY2)
                    raw2[2 * part + k, to, :] = full[p * NY2 : (p + 1) * NY2]
    level2.build(-9, 20, -10, 24)
    arrived(LOW_RHS, rg2)
    for n, (i, j) in enumerate(BALL):
        for p in range(NX2):
            rhs2[0, pl.ds(row2(p - 2 * i, -4 * j), NY2), :] = rg2[n, pl.ds(p * NY2, NY2), :]
    coarse = chebyshev_weights(COARSE_SWEEPS)
    level2.first_from_zero(coarse[0], (it2_a, 0), -10, 22, -10, 24)
    src, dst = it2_a, it2_b
    for sweep in range(1, COARSE_SWEEPS):
        reach = COARSE_SWEEPS - 1 - sweep
        first_y, rows = (-10, 24) if reach > 3 else (-6, 16)
        level2.sweep(coarse[sweep], (src, 0), (dst, 0), -3 - reach, 8 + 2 * reach, first_y, rows, last=reach == 0)
        src, dst = dst, src

    def store_it1(to, value):
        it1_b[0, pl.ds(to, NY1), :] = value

    arrived(MID_ITER, rx1)
    mid_unpack(rx1, store_it1)

    def lift1(big):
        stores = []
        for y in (-3, -1):
            value = src[0, pl.ds(row2(big, y), 8), :]
            for p in range(2):
                for q in range(2):
                    to = pl.ds(row1(2 * big + p, 2 * y + q), 8, stride=2)
                    stores.append((it1_a, (0, to), it1_b[0, to, :] + value))
        return stores

    plane_loop(-3, 8, lift1)
    level1.sweep(weights[0], (it1_a, 0), (it1_b, 0), -5, 14, -8, 24)
    level1.sweep(weights[1], (it1_b, 0), (it1_a, 0), -4, 12, -8, 24)
    level1.sweep(weights[2], (it1_a, 0), (it1_b, 0), -3, 10, -4, 16)
    level1.sweep(weights[3], (it1_b, 0), (it1_a, 0), -2, 8, -4, 16, last=True)

    arrived(FINE_ITER, riu)
    unpack(fine_b, 0, 2, riu, PLAN_U, 4, 4)

    def lift0(big):
        stores = []
        for y in (-2, 2):
            value = it1_a[0, pl.ds(row1(big, y), 8), :]
            for e in range(2):
                for p in range(2):
                    for q in range(2):
                        to = pl.ds(row0(2 * big + p, 2 * y + q), 8, stride=2)
                        stores.append((fine_a, (e, to), fine_b[e, to, :] + value))
        return stores

    plane_loop(-2, 8, lift0)
    level0.sweep(weights[0], (fine_a, 0), (fine_b, 0), -3, 14, -4, 24)
    level0.sweep(weights[1], (fine_b, 0), (fine_a, 0), -2, 12, -4, 24)
    level0.sweep(weights[2], (fine_a, 0), (fine_b, 0), -1, 10, -4, 24)
    back = HALF * ((at // 2) % 2) + at // 4
    even = (at % 2) == 0

    def emit(x, news):
        stores = []
        for half in range(2):
            pick = back + 32 * half
            lower = jnp.take_along_axis(news[0], pick, axis=1, mode="promise_in_bounds")
            upper = jnp.take_along_axis(news[1], pick, axis=1, mode="promise_in_bounds")
            stores.append((out_v, (x, slice(None), slice(half * LANES, (half + 1) * LANES)), jnp.where(even, lower, upper)))
        return stores

    level0.sweep(weights[3], (fine_b, 0), None, 0, 8, 0, NY0, last=True, emit=emit)
    store = pltpu.make_async_copy(out_v, out_hbm, out_sem.at[0])
    store.start()
    for group, landing in enumerate((rra, rrb, rmc, r2c, rg1, rg2, rx1, riu)):
        departed(group, landing)
    store.wait()


def solution(mesh):
    counts = (mesh.shape["gx"], mesh.shape["gy"])

    def local(source, initial, absorption, beta_x, beta_y, beta_z):
        f32 = jnp.float32
        v = lambda *shape: pltpu.VMEM(shape, f32)
        scratch = [
            v(6, NX0, NY0, 256), v(12, ROWS0, LANES), v(2, ROWS0, LANES), v(2, ROWS0, LANES),
            v(12, ROWS0, LANES), v(2, ROWS0, LANES), v(2, ROWS0, LANES), v(2, ROWS0, LANES), v(2, 128, LANES),
            v(4, ROWS1, LANES), v(6, ROWS1, LANES), v(1, ROWS1, LANES), v(1, ROWS1, LANES), v(1, ROWS1, LANES),
            v(1, ROWS1, LANES), v(1, ROWS1, LANES), v(32, LANES),
            v(4, ROWS2, LANES), v(6, ROWS2, LANES), v(1, ROWS2, LANES), v(1, ROWS2, LANES), v(1, ROWS2, LANES),
            v(1, ROWS2, LANES), v(1, ROWS2, LANES),
            v(SIZE_A, LANES), v(SIZE_A, LANES), v(SIZE_B, LANES), v(SIZE_B, LANES),
            v(4, 32, LANES), v(44, 32, LANES), v(4, 8, LANES), v(44, 8, LANES), v(4, 8, LANES), v(44, 8, LANES),
            v(16, LANES), v(len(BALL), 16, LANES), v(8, LANES), v(len(BALL), 8, LANES),
            v(SIZE_U, LANES), v(SIZE_U, LANES), v(NX0, NY0, 256),
            pltpu.SemaphoreType.DMA((6,)), pltpu.SemaphoreType.DMA((1,)),
            pltpu.SemaphoreType.DMA((8,)), pltpu.SemaphoreType.DMA((8,)),
        ]
        call = pl.pallas_call(
            lambda *refs: kernel(counts, *refs),
            out_shape=jax.ShapeDtypeStruct((NX0, NY0, 256), f32),
            in_specs=[pl.BlockSpec(memory_space=pl.ANY)] * 6,
            out_specs=pl.BlockSpec(memory_space=pl.ANY),
            scratch_shapes=scratch,
            compiler_params=pltpu.CompilerParams(
                collective_id=0, has_side_effects=True, vmem_limit_bytes=56 * 2**20
            ),
            name="vcycle",
        )
        return call(absorption, beta_x, beta_y, beta_z, source, initial)

    return jax.shard_map(
        local,
        mesh=mesh,
        in_specs=(P("gx", "gy", None),) * 6,
        out_specs=P("gx", "gy", None),
        check_vma=False,
    )
```

time: 71.4 us -> 64.6 us (0.905)
  Pallas kernels: 69.7 us -> 62.9 us
    pallas_call x1, Pallas kernels: 69.7 us -> 62.9 us  [local(): return call(absorption, beta_x, beta_y, beta_z, source, initial)]
where the time goes in v2:
time: 64.6 us; the launch traced here: 64.5 us
  Pallas kernels  62.9 us (97%)
  local copies, waits for them, and re-layouts  1.57 us (2%)
    pallas_call x1, Pallas kernels, local(): return call(absorption, beta_x, beta_y, beta_z, source, initial)  62.9 us
    unnamed x1, local copies, waits for them, and re-layouts  1.57 us

profile of v2, /device:TPU:1, one launch (start us, length us, event | category | flops | bytes accessed | tf_op | source)
XLA Modules:
  0.0 64.5 jit_solution(16340413443448936642)
XLA Ops:
  0.0 62.9 %vcycle.1 = f32[8,16,256]{2,1,0:T(8,128)} custom-call(f32[8,16,256]{2,1,0:T(8,128)} %refs_0_.1, f32[8,16,256]{2,1,0:T(8,128)} %refs_1_.1, f32[8,16,256]{2,1,0:T(8,128)} %refs_2_.1, f32[8,16,256]{2,1,0:T(8,128)} %refs_3_.1, f32[8,16,256]{2,1,0:T(8,128)} %refs_4_.1, f32[8,16,256]{2,1,0:T(8,128)} %refs_5_.1), custom_call_target="tpu_custom_call" | custom-call | tf_op jit(solution)/shard_map/vcycle/pallas_call | solution.py:625
  62.9 1.6 %copy.8 = f32[8,16,256]{2,1,0:T(8,128)} copy(f32[8,16,256]{2,1,0:T(8,128)} %vcycle.1) | data formatting | bytes 262144

commit v3 on v2

--- a/solution.py
+++ b/solution.py
@@ -22,7 +22,8 @@
 DEPTH = 5
 NEAR = [(-1, 0), (1, 0), (0, -1), (0, 1), (-1, -1), (-1, 1), (1, -1), (1, 1)]
 WIDE = [(-2, 0), (2, 0), (-2, -1), (-2, 1), (2, -1), (2, 1)]
-MIDS = NEAR + WIDE
+LINE = [1, -1, 2, -2, 3, -3, 4, -4, 5, -5]
+COLUMNS = [(-1, 11), (1, 11), (-2, 7), (2, 7), (-3, 3), (3, 3)]
 
 
 def ball_offsets():
@@ -235,7 +236,31 @@
     return depth * (depth - 1) // 2
 
 
-RAW_A, RAW_B, MID_COEF, LOW_COEF, MID_RHS, LOW_RHS, MID_ITER, FINE_ITER = range(8)
+def mid_corner(sx, sy):
+    for dx in range(1, NX1 + 1):
+        rows = 7 - dx
+        yield (NX1 - dx if sx > 0 else dx - 1), (NY1 - rows if sy > 0 else 0), rows
+
+
+def mid_plan(fields):
+    sizes = [fields * NX1 * NY1] * 4 + [-(-fields * 18 // 8) * 8] * 4
+    return list(zip([sum(sizes[:n]) for n in range(8)], sizes)), sum(sizes)
+
+
+def wide_pieces(sx, sy):
+    for dx in range(2):
+        x = NX1 - 1 - dx if sx > 0 else dx
+        if sy == 0:
+            yield x, 0, NY1
+        else:
+            yield x, (NY1 - 2 if sy > 0 else 0), 2
+
+
+WIDE_SIZES = [96, 96, 24, 24, 24, 24]
+WIDE_STARTS = [sum(WIDE_SIZES[:n]) for n in range(6)]
+RAW_A, RAW_B, LOW_LINE, MID_COEF, MID_RHS, LOW_COEF, LOW_RHS, MID_ITER, MID_WIDE, FINE_ITER = range(10)
+PLAN_M4, SIZE_M4 = mid_plan(4)
+PLAN_M1, SIZE_M1 = mid_plan(1)
 PLAN_A, SIZE_A = near_plan(8, 4, DEPTH, (32, 0))
 PLAN_B, SIZE_B = near_plan(4, 4, DEPTH, (32, 32))
 PLAN_U, SIZE_U = near_plan(2, 4, 4)
@@ -246,7 +271,7 @@
     (nat, fine, fine_a, fine_b, coef0, diag0, rhs0, upd0, rest0,
      raw1, coef1, diag1, rhs1, upd1, it1_a, it1_b, rest1,
      raw2, coef2, diag2, rhs2, upd2, it2_a, it2_b,
-     sra, rra, srb, rrb, smc, rmc, sg1, rg1, sx1, rx1, s2c, r2c, sg2, rg2, siu, riu, out_v,
+     sra, rra, srb, rrb, smc, cmc, rmc, sg1, cg1, rg1, sx1, cx1, rx1, r2l, r2c, sg2, rg2, siu, riu, swi, rwi, out_v,
      in_sem, out_sem, sent, got) = refs[7:]
     count_x, count_y = counts
     me_x, me_y = lax.axis_index("gx"), lax.axis_index("gy")
@@ -381,27 +406,28 @@
         face_z = sum(children(3, 0, x + p, q) for p in range(2) for q in range(2)) * 0.25
         for k, value in enumerate((absorb, face_x, face_y, face_z)):
             raw1[k, to, :] = value
-            smc[big, pl.ds(k * NY1, NY1), :] = value
+            smc[pl.ds(k * 32 + big * NY1, NY1), :] = value
 
     for big in range(NX1):
         coarsen1(big)
 
-    def mid_sends(group, src, landing):
-        for n, offset in enumerate(MIDS):
-            if n < 8:
-                send(group, src, landing.at[pl.ds(4 * n, 4)], offset)
-            else:
-                cut = pl.ds(2 if offset[0] > 0 else 0, 2)
-                send(group, src.at[cut], landing.at[pl.ds(16 + 2 * n, 2)], offset)
-
-    mid_sends(MID_COEF, smc, rmc)
-
-    def mid_unpack(landing, store):
-        for n, (sx, sy) in enumerate(MIDS):
-            planes = range(4) if n < 8 else (range(2, 4) if sx > 0 else range(2))
-            first = 4 * n if n < 8 else 16 + 2 * n
-            for i, x in enumerate(planes):
-                store(row1(x - sx * NX1, -sy * NY1), landing[first + i])
+    def mid_sends(group, own, corner, landing, plan, fields):
+        for n, offset in enumerate(NEAR[4:]):
+            to = 0
+            for k in range(fields):
+                for x, y, rows in mid_corner(*offset):
+                    corner[n, pl.ds(to, rows), :] = own[pl.ds(k * 32 + x * NY1 + y, rows), :]
+                    to += rows
+        for n, ((start, rows), offset) in enumerate(zip(plan, NEAR)):
+            send(group, own if n < 4 else corner.at[n - 4], landing.at[pl.ds(start, rows)], offset)
+
+    def mid_unpack(landing, plan, fields, store):
+        for n, ((start, _), (sx, sy)) in enumerate(zip(plan, NEAR)):
+            for k in range(fields):
+                pieces = mid_corner(sx, sy) if n >= 4 else ((x, 0, NY1) for x in range(NX1))
+                for x, y, rows in pieces:
+                    store(k, pl.ds(row1(x - sx * NX1, y - sy * NY1), rows), landing[pl.ds(start, rows), :])
+                    start += rows
 
     def both(v):
         return v + pltpu.roll(v, HALF, 1)
@@ -417,14 +443,16 @@
         face_z = jnp.where(low, face_z, pltpu.roll(face_z, HALF, 1))
         for k, value in enumerate((absorb, face_x, face_y, face_z)):
             raw2[k, pl.ds(row2(big, 0), NY2), :] = value
-        s2c[pl.ds(big * NY2, NY2), :] = jnp.where(low, absorb, face_x)
-        s2c[pl.ds(8 + big * NY2, NY2), :] = jnp.where(low, face_y, face_z)
+        r2l[0, pl.ds(big * NY2, NY2), :] = jnp.where(low, absorb, face_x)
+        r2l[0, pl.ds(8 + big * NY2, NY2), :] = jnp.where(low, face_y, face_z)
 
     def ball_sends(group, src, landing):
         for n, offset in enumerate(BALL):
             send(group, src, landing.at[n], offset)
 
-    ball_sends(LOW_COEF, s2c, r2c)
+    for n, i in enumerate(LINE):
+        send(LOW_LINE, r2l.at[0], r2l.at[n + 1], (i, 0))
+    mid_sends(MID_COEF, smc, cmc, rmc, PLAN_M4, 4)
 
     arrived(RAW_A, rra)
     unpack(fine, 0, 8, rra, PLAN_A, 4, DEPTH)
@@ -452,12 +480,11 @@
     raw1[1, pl.ds(row1(NX1, 0), NY1), :] = face_x
     arrived(MID_COEF, rmc)
 
-    def store_raw(to, value):
-        for k in range(4):
-            raw1[k, pl.ds(to, NY1), :] = value[k * NY1 : (k + 1) * NY1]
-
-    mid_unpack(rmc, store_raw)
-    level1.build(-5, 14, -8, 24)
+    def store_raw(k, to, value):
+        raw1[k, to, :] = value
+
+    mid_unpack(rmc, PLAN_M4, 4, store_raw)
+    level1.build(-4, 11, -8, 24)
     for big in range(NX1):
         total = sum(
             rest0[e, pl.ds((2 * big + p) * NY0 + q, NY1, stride=2), :]
@@ -465,9 +492,14 @@
         )
         value = total * 0.125 / diag1[0, pl.ds(row1(big, 0), NY1), :]
         rhs1[0, pl.ds(row1(big, 0), NY1), :] = value
-        sg1[big] = value
-
-    mid_sends(MID_RHS, sg1, rg1)
+        sg1[pl.ds(big * NY1, NY1), :] = value
+
+    mid_sends(MID_RHS, sg1, cg1, rg1, PLAN_M1, 1)
+    arrived(LOW_LINE, r2l.at[pl.ds(1, 10)])
+    start = 0
+    for j, slots in COLUMNS:
+        send(LOW_COEF, r2l.at[pl.ds(0, slots)], r2c.at[pl.ds(start, slots)], (0, j))
+        start += slots
 
     x = NX1
     grand = lambda k, x, y: raw1[k, pl.ds(row1(x, y), NY2, stride=2), :]
@@ -477,11 +509,11 @@
         raw2[2, pl.ds(row2(big, NY2), 1), :] = above[0:1]
     diag_own2 = [level2.own_diagonal(big, 0, NY2)[0] for big in range(NX2)]
 
-    def store_rhs1(to, value):
-        rhs1[0, pl.ds(to, NY1), :] = value
+    def store_rhs1(k, to, value):
+        rhs1[0, to, :] = value
 
     arrived(MID_RHS, rg1)
-    mid_unpack(rg1, store_rhs1)
+    mid_unpack(rg1, PLAN_M1, 1, store_rhs1)
     level1.first_from_zero(weights[0], (it1_a, 0), -4, 12, -4, 16)
     level1.sweep(weights[1], (it1_a, 0), (it1_b, 0), -3, 10, -4, 16)
     level1.sweep(weights[2], (it1_b, 0), (it1_a, 0), -2, 8, -4, 16)
@@ -492,36 +524,59 @@
         steps, centre = level1.residual((it1_b, 0), at_row, NY1)
         return [
             (rest1, (pl.ds(x * NY1, NY1),), steps[0] * diag1[0, pl.ds(at_row, NY1), :]),
-            (sx1, (x,), centre[0]),
+            (sx1, (pl.ds(x * NY1, NY1),), centre[0]),
         ]
 
     plane_loop(0, NX1, rest_mid)
+    rhs_own2 = []
     for big in range(NX2):
         total = sum(rest1[pl.ds((2 * big + p) * NY1 + q, NY2, stride=2), :] for p in range(2) for q in range(2))
-        value = both(total) * 0.125 / diag_own2[big]
-        rhs2[0, pl.ds(row2(big, 0), NY2), :] = value
-        sg2[pl.ds(big * NY2, NY2), :] = value
+        rhs_own2.append(both(total) * 0.125 / diag_own2[big])
+        rhs2[0, pl.ds(row2(big, 0), NY2), :] = rhs_own2[big]
+    sg2[...] = jnp.where(low, rhs_own2[0], rhs_own2[1])
 
     ball_sends(LOW_RHS, sg2, rg2)
-    mid_sends(MID_ITER, sx1, rx1)
+    mid_sends(MID_ITER, sx1, cx1, rx1, PLAN_M1, 1)
     pack(fine_b, 0, 2, siu, PLAN_U, 4, 4)
     near_sends(FINE_ITER, siu, riu, PLAN_U)
+    for n, offset in enumerate(WIDE):
+        to = WIDE_STARTS[n]
+        for k in range(6):
+            own, base = ((smc, 32 * k), (sg1, 0), (sx1, 0))[max(k - 3, 0)]
+            for x, y, rows in wide_pieces(*offset):
+                swi[pl.ds(to, rows), :] = own[pl.ds(base + x * NY1 + y, rows), :]
+                to += rows
+        cut = pl.ds(WIDE_STARTS[n], WIDE_SIZES[n])
+        send(MID_WIDE, swi.at[cut], rwi.at[cut], offset)
 
     arrived(LOW_COEF, r2c)
     low8 = lanes((8, LANES)) < HALF
-    for n, (i, j) in enumerate(BALL):
+
+    def two_fields(value):
+        other = pltpu.roll(value, HALF, 1)
+        return jnp.where(low8, value, other), jnp.where(low8, other, value)
+
+    def low_unpack(ref, slot, i, j):
         for part in range(2):
-            value = r2c[n, pl.ds(8 * part, 8), :]
-            other = pltpu.roll(value, HALF, 1)
-            for k, full in enumerate((jnp.where(low8, value, other), jnp.where(low8, other, value))):
+            for k, full in enumerate(two_fields(ref[slot, pl.ds(8 * part, 8), :])):
                 for p in range(NX2):
                     to = pl.ds(row2(p - 2 * i, -4 * j), NY2)
                     raw2[2 * part + k, to, :] = full[p * NY2 : (p + 1) * NY2]
+
+    for n, i in enumerate(LINE):
+        low_unpack(r2l, n + 1, i, 0)
+    start = 0
+    for j, slots in COLUMNS:
+        for n, i in enumerate(([0] + LINE)[:slots]):
+            low_unpack(r2c, start + n, i, j)
+        start += slots
     level2.build(-9, 20, -10, 24)
     arrived(LOW_RHS, rg2)
     for n, (i, j) in enumerate(BALL):
-        for p in range(NX2):
-            rhs2[0, pl.ds(row2(p - 2 * i, -4 * j), NY2), :] = rg2[n, pl.ds(p * NY2, NY2), :]
+        value = rg2[n]
+        other = pltpu.roll(value, HALF, 1)
+        rhs2[0, pl.ds(row2(-2 * i, -4 * j), NY2), :] = jnp.where(low, value, other)
+        rhs2[0, pl.ds(row2(1 - 2 * i, -4 * j), NY2), :] = jnp.where(low, other, value)
     coarse = chebyshev_weights(COARSE_SWEEPS)
     level2.first_from_zero(coarse[0], (it2_a, 0), -10, 22, -10, 24)
     src, dst = it2_a, it2_b
@@ -531,11 +586,21 @@
         level2.sweep(coarse[sweep], (src, 0), (dst, 0), -3 - reach, 8 + 2 * reach, first_y, rows, last=reach == 0)
         src, dst = dst, src
 
-    def store_it1(to, value):
-        it1_b[0, pl.ds(to, NY1), :] = value
+    def store_it1(k, to, value):
+        it1_b[0, to, :] = value
 
     arrived(MID_ITER, rx1)
-    mid_unpack(rx1, store_it1)
+    mid_unpack(rx1, PLAN_M1, 1, store_it1)
+    arrived(MID_WIDE, rwi)
+    for n, (sx, sy) in enumerate(WIDE):
+        start = WIDE_STARTS[n]
+        for k in range(6):
+            ref, field = (raw1, k) if k < 4 else ((rhs1, 0) if k == 4 else (it1_b, 0))
+            for x, y, rows in wide_pieces(sx, sy):
+                ref[field, pl.ds(row1(x - sx * NX1, y - sy * NY1), rows), :] = rwi[pl.ds(start, rows), :]
+                start += rows
+    level1.build(-5, 1, -8, 24)
+    level1.build(7, 2, -8, 24)
 
     def lift1(big):
         stores = []
@@ -586,7 +651,7 @@
     level0.sweep(weights[3], (fine_b, 0), None, 0, 8, 0, NY0, last=True, emit=emit)
     store = pltpu.make_async_copy(out_v, out_hbm, out_sem.at[0])
     store.start()
-    for group, landing in enumerate((rra, rrb, rmc, r2c, rg1, rg2, rx1, riu)):
+    for group, landing in enumerate((rra, rrb, r2l.at[pl.ds(1, 10)], rmc, rg1, r2c, rg2, rx1, rwi, riu)):
         departed(group, landing)
     store.wait()
 
@@ -605,11 +670,12 @@
             v(4, ROWS2, LANES), v(6, ROWS2, LANES), v(1, ROWS2, LANES), v(1, ROWS2, LANES), v(1, ROWS2, LANES),
             v(1, ROWS2, LANES), v(1, ROWS2, LANES),
             v(SIZE_A, LANES), v(SIZE_A, LANES), v(SIZE_B, LANES), v(SIZE_B, LANES),
-            v(4, 32, LANES), v(44, 32, LANES), v(4, 8, LANES), v(44, 8, LANES), v(4, 8, LANES), v(44, 8, LANES),
-            v(16, LANES), v(len(BALL), 16, LANES), v(8, LANES), v(len(BALL), 8, LANES),
-            v(SIZE_U, LANES), v(SIZE_U, LANES), v(NX0, NY0, 256),
+            v(128, LANES), v(4, 72, LANES), v(SIZE_M4, LANES),
+            v(32, LANES), v(4, 24, LANES), v(SIZE_M1, LANES), v(32, LANES), v(4, 24, LANES), v(SIZE_M1, LANES),
+            v(11, 16, LANES), v(42, 16, LANES), v(NY2, LANES), v(len(BALL), NY2, LANES),
+            v(SIZE_U, LANES), v(SIZE_U, LANES), v(288, LANES), v(288, LANES), v(NX0, NY0, 256),
             pltpu.SemaphoreType.DMA((6,)), pltpu.SemaphoreType.DMA((1,)),
-            pltpu.SemaphoreType.DMA((8,)), pltpu.SemaphoreType.DMA((8,)),
+            pltpu.SemaphoreType.DMA((10,)), pltpu.SemaphoreType.DMA((10,)),
         ]
         call = pl.pallas_call(
             lambda *refs: kernel(counts, *refs),

time: 64.6 us -> 56.6 us (0.88)
  Pallas kernels: 62.9 us -> 54.9 us
    pallas_call x1, Pallas kernels: 62.9 us -> 54.9 us  [local(): return call(absorption, beta_x, beta_y, beta_z, source, initial)]
where the time goes in v3:
time: 56.6 us; the launch traced here: 56.5 us
  Pallas kernels  54.9 us (97%)
  local copies, waits for them, and re-layouts  1.57 us (3%)
    pallas_call x1, Pallas kernels, local(): return call(absorption, beta_x, beta_y, beta_z, source, initial)  54.9 us
    unnamed x1, local copies, waits for them, and re-layouts  1.57 us

profile of v3, /device:TPU:1, one launch (start us, length us, event | category | flops | bytes accessed | tf_op | source)
XLA Modules:
  0.0 56.5 jit_solution(39093771765814272)
XLA Ops:
  0.0 54.9 %vcycle.1 = f32[8,16,256]{2,1,0:T(8,128)} custom-call(f32[8,16,256]{2,1,0:T(8,128)} %refs_0_.1, f32[8,16,256]{2,1,0:T(8,128)} %refs_1_.1, f32[8,16,256]{2,1,0:T(8,128)} %refs_2_.1, f32[8,16,256]{2,1,0:T(8,128)} %refs_3_.1, f32[8,16,256]{2,1,0:T(8,128)} %refs_4_.1, f32[8,16,256]{2,1,0:T(8,128)} %refs_5_.1), custom_call_target="tpu_custom_call" | custom-call | tf_op jit(solution)/shard_map/vcycle/pallas_call | solution.py:691
  54.9 1.6 %copy.8 = f32[8,16,256]{2,1,0:T(8,128)} copy(f32[8,16,256]{2,1,0:T(8,128)} %vcycle.1) | data formatting | bytes 262144

commit v4 on v3

--- a/solution.py
+++ b/solution.py
@@ -19,7 +19,7 @@
 ROWS1 = 416
 ROWS2 = 616
 
-DEPTH = 5
+DEPTH = 4
 NEAR = [(-1, 0), (1, 0), (0, -1), (0, 1), (-1, -1), (-1, 1), (1, -1), (1, 1)]
 WIDE = [(-2, 0), (2, 0), (-2, -1), (-2, 1), (2, -1), (2, 1)]
 LINE = [1, -1, 2, -2, 3, -3, 4, -4, 5, -5]
@@ -160,7 +160,7 @@
 
         plane_loop(first_x, count, body)
 
-    def residual(self, src, at, rows):
+    def stencil(self, src, at, rows):
         n = self.halves
         ref, base = src
         take = lambda e, shift=0: ref[base + e, pl.ds(at + shift, rows), :]
@@ -169,12 +169,37 @@
         out = []
         for e in range(n):
             c = lambda k: self.coef[k * n + e, pl.ds(at, rows), :]
-            t = self.rhs[e, pl.ds(at, rows), :] - centre[e]
             t_x = c(0) * take(e, -self.pitch) + c(1) * take(e, self.pitch)
             t_y = c(2) * take(e, -1) + c(3) * take(e, 1)
             t_z = c(4) * below[e] + c(5) * above[e]
-            out.append(t + (t_x + t_y) + t_z)
+            out.append((t_x + t_y) + t_z)
         return out, centre
+
+    def residual(self, src, at, rows):
+        sums, centre = self.stencil(src, at, rows)
+        return [(self.rhs[e, pl.ds(at, rows), :] - centre[e]) + sums[e] for e in range(self.halves)], centre
+
+    def advance(self, pair, src, dst, old, new, total, first_x, count, first_y, rows, lead=1.0, lift=False, emit=None):
+        def body(x):
+            at = self.row(x, first_y)
+            here = pl.ds(at, rows)
+            sums, centre = self.stencil((src, 0), at, rows)
+            stores, news = [], []
+            for e in range(self.halves):
+                change = centre[e] - sums[e]
+                rest = old[e, here, :] - (change if lead == 1.0 else lead * change)
+                step = pair[1] * rest
+                if pair[0] != 0.0:
+                    step = (pair[0] * lead) * centre[e] + step
+                iterate = total[e, here, :] + step
+                if lift:
+                    iterate = iterate + centre[e]
+                news.append(iterate)
+                if emit is None:
+                    stores += [(new, (e, here), rest), (dst, (e, here), step), (total, (e, here), iterate)]
+            return stores if emit is None else emit(x, news)
+
+        plane_loop(first_x, count, body)
 
     def sweep(self, pair, src, dst, first_x, count, first_y, rows, last=False, emit=None):
         def body(x):
@@ -258,20 +283,21 @@
 
 WIDE_SIZES = [96, 96, 24, 24, 24, 24]
 WIDE_STARTS = [sum(WIDE_SIZES[:n]) for n in range(6)]
-RAW_A, RAW_B, LOW_LINE, MID_COEF, MID_RHS, LOW_COEF, LOW_RHS, MID_ITER, MID_WIDE, FINE_ITER = range(10)
+FIRST, RAW, FINE_REST, LOW_LINE, MID_COEF, MID_RHS, LOW_COEF, LOW_RHS, MID_ITER, MID_WIDE, FINE_BACK = range(11)
 PLAN_M4, SIZE_M4 = mid_plan(4)
 PLAN_M1, SIZE_M1 = mid_plan(1)
-PLAN_A, SIZE_A = near_plan(8, 4, DEPTH, (32, 0))
-PLAN_B, SIZE_B = near_plan(4, 4, DEPTH, (32, 32))
-PLAN_U, SIZE_U = near_plan(2, 4, 4)
+PLAN_F, SIZE_F = [(0, 64), (64, 32), (96, 32), (128, 16)], 144
+PLAN_A, SIZE_A = near_plan(8, 3, DEPTH, (32, 0))
+PLAN_T, SIZE_T = near_plan(2, 4, DEPTH)
+PLAN_U, SIZE_U = near_plan(2, 3, 3)
 
 
 def kernel(counts, *refs):
     inputs, out_hbm = refs[:6], refs[6]
-    (nat, fine, fine_a, fine_b, coef0, diag0, rhs0, upd0, rest0,
+    (nat, fine, fine_a, fine_b, coef0, diag0, rhs0, rest_a, rest_b, total0, rest0,
      raw1, coef1, diag1, rhs1, upd1, it1_a, it1_b, rest1,
      raw2, coef2, diag2, rhs2, upd2, it2_a, it2_b,
-     sra, rra, srb, rrb, smc, cmc, rmc, sg1, cg1, rg1, sx1, cx1, rx1, r2l, r2c, sg2, rg2, siu, riu, swi, rwi, out_v,
+     sfi, rfi, sra, rra, sta, rta, smc, cmc, rmc, sg1, cg1, rg1, sx1, cx1, rx1, r2l, r2c, sg2, rg2, siu, riu, swi, rwi, out_v,
      in_sem, out_sem, sent, got) = refs[7:]
     count_x, count_y = counts
     me_x, me_y = lax.axis_index("gx"), lax.axis_index("gy")
@@ -298,7 +324,7 @@
     def departed(group, landing):
         pltpu.make_async_copy(landing, landing, sent.at[group]).wait()
 
-    level0 = Level(0, 2, row0, YP0, fine, coef0, diag0, rhs0, upd0)
+    level0 = Level(0, 2, row0, YP0, fine, coef0, diag0, rhs0, None)
     level1 = Level(1, 1, row1, YP1, raw1, coef1, diag1, rhs1, upd1)
     level2 = Level(2, 1, row2, YP2, raw2, coef2, diag2, rhs2, upd2)
 
@@ -380,19 +406,32 @@
             cut = pl.ds(start, rows)
             send(group, out.at[cut], landing.at[cut], offset)
 
-    for k in range(4):
+    def first_pieces():
+        for n, (sx, sy) in enumerate(NEAR[:4]):
+            fields = (10, 11) + ((2, 3) if n == 0 else (4, 5) if n == 2 else ())
+            for i, k in enumerate(fields):
+                shift = -(sx * NX0 * YP0 + sy * NY0)
+                if n < 2:
+                    yield k, row0(side_plane(sx, 1), 0), NY0, None, shift, PLAN_F[n][0] + i * NY0
+                else:
+                    yield k, row0(0, side_row(sy, 1)), NX0, YP0, shift, PLAN_F[n][0] + i * NX0
+
+    weights = chebyshev_weights(SWEEPS)
+    for k in (5, 1, 2):
         loads[k].wait()
         permute(k)
-    pack(fine, 0, 8, sra, PLAN_A, 4, DEPTH)
-    extra_out(fine, 2, sra, PLAN_A, 512, (0,))
+    for k, row, rows, stride, _, to in first_pieces():
+        sfi[pl.ds(to, rows), :] = fine[k, pl.ds(row, rows, stride=stride), :]
     pl.semaphore_wait(barrier, len(BALL))
-    near_sends(RAW_A, sra, rra, PLAN_A)
-    for k in (4, 5):
+    near_sends(FIRST, sfi, rfi, PLAN_F)
+    for k in (0, 3):
         loads[k].wait()
         permute(k)
-    pack(fine, 8, 4, srb, PLAN_B, 4, DEPTH)
-    extra_out(fine, 10, srb, PLAN_B, 256, (0, 1))
-    near_sends(RAW_B, srb, rrb, PLAN_B)
+    pack(fine, 0, 8, sra, PLAN_A, 3, DEPTH)
+    extra_out(fine, 2, sra, PLAN_A, 384, (0,))
+    near_sends(RAW, sra, rra, PLAN_A)
+    loads[4].wait()
+    permute(4)
 
     def children(k, e, x, y_step):
         return fine[2 * k + e, pl.ds(row0(x, y_step), NY1, stride=2), :]
@@ -450,57 +489,32 @@
         for n, offset in enumerate(BALL):
             send(group, src, landing.at[n], offset)
 
+    arrived(FIRST, rfi)
+    for k, row, rows, stride, shift, at_buffer in first_pieces():
+        fine[k, pl.ds(row + shift, rows, stride=stride), :] = rfi[pl.ds(at_buffer, rows), :]
+    level0.build(0, NX0, 0, NY0, (fine, 8))
+
+    def first_sweep(x):
+        here = pl.ds(row0(x, 0), NY0)
+        steps, centre = level0.residual((fine, 10), row0(x, 0), NY0)
+        stores = []
+        for e in range(2):
+            stores.append((rest_a, (e, here), steps[e]))
+            stores.append((total0, (e, here), centre[e] + weights[0][1] * steps[e]))
+        return stores
+
+    plane_loop(0, NX0, first_sweep)
+    pack(rest_a, 0, 2, sta, PLAN_T, 4, DEPTH)
+    near_sends(FINE_REST, sta, rta, PLAN_T)
     for n, i in enumerate(LINE):
         send(LOW_LINE, r2l.at[0], r2l.at[n + 1], (i, 0))
     mid_sends(MID_COEF, smc, cmc, rmc, PLAN_M4, 4)
 
-    arrived(RAW_A, rra)
-    unpack(fine, 0, 8, rra, PLAN_A, 4, DEPTH)
-    extra_in(fine, 2, rra, PLAN_A, 512, (0,))
-    arrived(RAW_B, rrb)
-    unpack(fine, 8, 4, rrb, PLAN_B, 4, DEPTH)
-    extra_in(fine, 10, rrb, PLAN_B, 256, (0, 1))
-    level0.build(-4, 16, -4, 24, (fine, 8))
-    weights = chebyshev_weights(SWEEPS)
-    level0.sweep(weights[0], (fine, 10), (fine_a, 0), -4, 16, -4, 24)
-    level0.sweep(weights[1], (fine_a, 0), (fine_b, 0), -3, 14, -4, 24)
-    level0.sweep(weights[2], (fine_b, 0), (fine_a, 0), -2, 12, -4, 24)
-    level0.sweep(weights[3], (fine_a, 0), (fine_b, 0), -1, 10, -4, 24, last=True)
-
-    def rest_fine(x):
-        at_row = row0(x, 0)
-        steps, _ = level0.residual((fine_b, 0), at_row, NY0)
-        return [
-            (rest0, (e, pl.ds(x * NY0, NY0)), steps[e] * diag0[e, pl.ds(at_row, NY0), :]) for e in range(2)
-        ]
-
-    plane_loop(0, NX0, rest_fine)
-
     face_x = sum(children(1, e, NX0, q) for e in range(2) for q in range(2)) * 0.25
     raw1[1, pl.ds(row1(NX1, 0), NY1), :] = face_x
-    arrived(MID_COEF, rmc)
-
-    def store_raw(k, to, value):
-        raw1[k, to, :] = value
-
-    mid_unpack(rmc, PLAN_M4, 4, store_raw)
-    level1.build(-4, 11, -8, 24)
-    for big in range(NX1):
-        total = sum(
-            rest0[e, pl.ds((2 * big + p) * NY0 + q, NY1, stride=2), :]
-            for e in range(2) for p in range(2) for q in range(2)
-        )
-        value = total * 0.125 / diag1[0, pl.ds(row1(big, 0), NY1), :]
-        rhs1[0, pl.ds(row1(big, 0), NY1), :] = value
-        sg1[pl.ds(big * NY1, NY1), :] = value
-
-    mid_sends(MID_RHS, sg1, cg1, rg1, PLAN_M1, 1)
-    arrived(LOW_LINE, r2l.at[pl.ds(1, 10)])
-    start = 0
-    for j, slots in COLUMNS:
-        send(LOW_COEF, r2l.at[pl.ds(0, slots)], r2c.at[pl.ds(start, slots)], (0, j))
-        start += slots
-
+    face_y = sum(fine[4 + e, pl.ds(row0(p, NY0), NX1, stride=2 * YP0), :] for e in range(2) for p in range(2)) * 0.25
+    raw1[2, pl.ds(row1(0, NY1), NX1, stride=YP1), :] = face_y
+    diag_own1 = [level1.own_diagonal(big, 0, NY1)[0] for big in range(NX1)]
     x = NX1
     grand = lambda k, x, y: raw1[k, pl.ds(row1(x, y), NY2, stride=2), :]
     raw2[1, pl.ds(row2(NX2, 0), NY2), :] = both(grand(1, x, 0) + grand(1, x, 1)) * 0.25
@@ -509,6 +523,51 @@
         raw2[2, pl.ds(row2(big, NY2), 1), :] = above[0:1]
     diag_own2 = [level2.own_diagonal(big, 0, NY2)[0] for big in range(NX2)]
 
+    arrived(RAW, rra)
+    unpack(fine, 0, 8, rra, PLAN_A, 3, DEPTH)
+    extra_in(fine, 2, rra, PLAN_A, 384, (0,))
+    level0.build(-3, 14, -4, 24)
+    arrived(FINE_REST, rta)
+    unpack(rest_a, 0, 2, rta, PLAN_T, 4, DEPTH)
+    level0.advance(weights[1], rest_a, fine_a, rest_a, rest_b, total0, -3, 14, -4, 24, lead=weights[0][1])
+    level0.advance(weights[2], fine_a, fine_b, rest_b, rest_b, total0, -2, 12, -4, 24)
+    level0.advance(weights[3], fine_b, fine_a, rest_b, rest_b, total0, -1, 10, -4, 24)
+
+    def rest_fine(x):
+        here = pl.ds(row0(x, 0), NY0)
+        sums, centre = level0.stencil((fine_a, 0), row0(x, 0), NY0)
+        stores = []
+        for e in range(2):
+            rest = rest_b[e, here, :] - (centre[e] - sums[e])
+            stores.append((rest_b, (e, here), rest))
+            stores.append((rest0, (e, pl.ds(x * NY0, NY0)), rest * diag0[e, here, :]))
+        return stores
+
+    plane_loop(0, NX0, rest_fine)
+    for big in range(NX1):
+        total = sum(
+            rest0[e, pl.ds((2 * big + p) * NY0 + q, NY1, stride=2), :]
+            for e in range(2) for p in range(2) for q in range(2)
+        )
+        value = total * 0.125 / diag_own1[big]
+        rhs1[0, pl.ds(row1(big, 0), NY1), :] = value
+        sg1[pl.ds(big * NY1, NY1), :] = value
+
+    mid_sends(MID_RHS, sg1, cg1, rg1, PLAN_M1, 1)
+    arrived(LOW_LINE, r2l.at[pl.ds(1, 10)])
+    start = 0
+    for j, slots in COLUMNS:
+        send(LOW_COEF, r2l.at[pl.ds(0, slots)], r2c.at[pl.ds(start, slots)], (0, j))
+        start += slots
+
+    arrived(MID_COEF, rmc)
+
+    def store_raw(k, to, value):
+        raw1[k, to, :] = value
+
+    mid_unpack(rmc, PLAN_M4, 4, store_raw)
+    level1.build(-4, 11, -8, 24)
+
     def store_rhs1(k, to, value):
         rhs1[0, to, :] = value
 
@@ -537,8 +596,8 @@
 
     ball_sends(LOW_RHS, sg2, rg2)
     mid_sends(MID_ITER, sx1, cx1, rx1, PLAN_M1, 1)
-    pack(fine_b, 0, 2, siu, PLAN_U, 4, 4)
-    near_sends(FINE_ITER, siu, riu, PLAN_U)
+    pack(rest_b, 0, 2, siu, PLAN_U, 3, 3)
+    near_sends(FINE_BACK, siu, riu, PLAN_U)
     for n, offset in enumerate(WIDE):
         to = WIDE_STARTS[n]
         for k in range(6):
@@ -618,8 +677,8 @@
     level1.sweep(weights[2], (it1_a, 0), (it1_b, 0), -3, 10, -4, 16)
     level1.sweep(weights[3], (it1_b, 0), (it1_a, 0), -2, 8, -4, 16, last=True)
 
-    arrived(FINE_ITER, riu)
-    unpack(fine_b, 0, 2, riu, PLAN_U, 4, 4)
+    arrived(FINE_BACK, riu)
+    unpack(rest_b, 0, 2, riu, PLAN_U, 3, 3)
 
     def lift0(big):
         stores = []
@@ -629,13 +688,13 @@
                 for p in range(2):
                     for q in range(2):
                         to = pl.ds(row0(2 * big + p, 2 * y + q), 8, stride=2)
-                        stores.append((fine_a, (e, to), fine_b[e, to, :] + value))
+                        stores.append((fine_b, (e, to), value))
         return stores
 
     plane_loop(-2, 8, lift0)
-    level0.sweep(weights[0], (fine_a, 0), (fine_b, 0), -3, 14, -4, 24)
-    level0.sweep(weights[1], (fine_b, 0), (fine_a, 0), -2, 12, -4, 24)
-    level0.sweep(weights[2], (fine_a, 0), (fine_b, 0), -1, 10, -4, 24)
+    level0.advance((0.0, weights[0][1]), fine_b, fine_a, rest_b, rest_b, total0, -3, 14, -4, 24, lift=True)
+    level0.advance(weights[1], fine_a, fine_b, rest_b, rest_b, total0, -2, 12, -4, 24)
+    level0.advance(weights[2], fine_b, fine_a, rest_b, rest_b, total0, -1, 10, -4, 24)
     back = HALF * ((at // 2) % 2) + at // 4
     even = (at % 2) == 0
 
@@ -648,10 +707,10 @@
             stores.append((out_v, (x, slice(None), slice(half * LANES, (half + 1) * LANES)), jnp.where(even, lower, upper)))
         return stores
 
-    level0.sweep(weights[3], (fine_b, 0), None, 0, 8, 0, NY0, last=True, emit=emit)
+    level0.advance(weights[3], fine_a, None, rest_b, None, total0, 0, 8, 0, NY0, emit=emit)
     store = pltpu.make_async_copy(out_v, out_hbm, out_sem.at[0])
     store.start()
-    for group, landing in enumerate((rra, rrb, r2l.at[pl.ds(1, 10)], rmc, rg1, r2c, rg2, rx1, rwi, riu)):
+    for group, landing in enumerate((rfi, rra, rta, r2l.at[pl.ds(1, 10)], rmc, rg1, r2c, rg2, rx1, rwi, riu)):
         departed(group, landing)
     store.wait()
 
@@ -664,18 +723,19 @@
         v = lambda *shape: pltpu.VMEM(shape, f32)
         scratch = [
             v(6, NX0, NY0, 256), v(12, ROWS0, LANES), v(2, ROWS0, LANES), v(2, ROWS0, LANES),
-            v(12, ROWS0, LANES), v(2, ROWS0, LANES), v(2, ROWS0, LANES), v(2, ROWS0, LANES), v(2, 128, LANES),
+            v(12, ROWS0, LANES), v(2, ROWS0, LANES), v(2, ROWS0, LANES), v(2, ROWS0, LANES), v(2, ROWS0, LANES), v(2, ROWS0, LANES),
+            v(2, 128, LANES),
             v(4, ROWS1, LANES), v(6, ROWS1, LANES), v(1, ROWS1, LANES), v(1, ROWS1, LANES), v(1, ROWS1, LANES),
             v(1, ROWS1, LANES), v(1, ROWS1, LANES), v(32, LANES),
             v(4, ROWS2, LANES), v(6, ROWS2, LANES), v(1, ROWS2, LANES), v(1, ROWS2, LANES), v(1, ROWS2, LANES),
             v(1, ROWS2, LANES), v(1, ROWS2, LANES),
-            v(SIZE_A, LANES), v(SIZE_A, LANES), v(SIZE_B, LANES), v(SIZE_B, LANES),
+            v(SIZE_F, LANES), v(SIZE_F, LANES), v(SIZE_A, LANES), v(SIZE_A, LANES), v(SIZE_T, LANES), v(SIZE_T, LANES),
             v(128, LANES), v(4, 72, LANES), v(SIZE_M4, LANES),
             v(32, LANES), v(4, 24, LANES), v(SIZE_M1, LANES), v(32, LANES), v(4, 24, LANES), v(SIZE_M1, LANES),
             v(11, 16, LANES), v(42, 16, LANES), v(NY2, LANES), v(len(BALL), NY2, LANES),
             v(SIZE_U, LANES), v(SIZE_U, LANES), v(288, LANES), v(288, LANES), v(NX0, NY0, 256),
             pltpu.SemaphoreType.DMA((6,)), pltpu.SemaphoreType.DMA((1,)),
-            pltpu.SemaphoreType.DMA((10,)), pltpu.SemaphoreType.DMA((10,)),
+            pltpu.SemaphoreType.DMA((11,)), pltpu.SemaphoreType.DMA((11,)),
         ]
         call = pl.pallas_call(
             lambda *refs: kernel(counts, *refs),

time: 56.6 us -> 49.9 us (0.88)
  Pallas kernels: 54.9 us -> 48.2 us
    pallas_call x1, Pallas kernels: 54.9 us -> 48.2 us  [local(): return call(absorption, beta_x, beta_y, beta_z, source, initial)]
where the time goes in v4:
time: 49.9 us; the launch traced here: 49.8 us
  Pallas kernels  48.2 us (97%)
  local copies, waits for them, and re-layouts  1.57 us (3%)
    pallas_call x1, Pallas kernels, local(): return call(absorption, beta_x, beta_y, beta_z, source, initial)  48.2 us
    unnamed x1, local copies, waits for them, and re-layouts  1.57 us

profile of v4, /device:TPU:1, one launch (start us, length us, event | category | flops | bytes accessed | tf_op | source)
XLA Modules:
  0.0 49.8 jit_solution(1321437714208983802)
XLA Ops:
  0.0 48.2 %vcycle.1 = f32[8,16,256]{2,1,0:T(8,128)} custom-call(f32[8,16,256]{2,1,0:T(8,128)} %refs_0_.1, f32[8,16,256]{2,1,0:T(8,128)} %refs_1_.1, f32[8,16,256]{2,1,0:T(8,128)} %refs_2_.1, f32[8,16,256]{2,1,0:T(8,128)} %refs_3_.1, f32[8,16,256]{2,1,0:T(8,128)} %refs_4_.1, f32[8,16,256]{2,1,0:T(8,128)} %refs_5_.1), custom_call_target="tpu_custom_call" | custom-call | tf_op jit(solution)/shard_map/vcycle/pallas_call | solution.py:751
  48.2 1.6 %copy.8 = f32[8,16,256]{2,1,0:T(8,128)} copy(f32[8,16,256]{2,1,0:T(8,128)} %vcycle.1) | data formatting | bytes 262144

commit v5 on v4

--- a/solution.py
+++ b/solution.py
@@ -9,7 +9,7 @@
 COARSE_SWEEPS = 8
 LANES = 128
 HALF = 64
-GROUP = 4
+GROUP = 8
 MESH = pl.DeviceIdType.MESH
 
 NX0, NY0, HX0, HY0, YP0 = 8, 16, 5, 5, 26
@@ -560,6 +560,8 @@
         send(LOW_COEF, r2l.at[pl.ds(0, slots)], r2c.at[pl.ds(start, slots)], (0, j))
         start += slots
 
+    pack(rest_b, 0, 2, siu, PLAN_U, 3, 3)
+    near_sends(FINE_BACK, siu, riu, PLAN_U)
     arrived(MID_COEF, rmc)
 
     def store_raw(k, to, value):
@@ -596,8 +598,6 @@
 
     ball_sends(LOW_RHS, sg2, rg2)
     mid_sends(MID_ITER, sx1, cx1, rx1, PLAN_M1, 1)
-    pack(rest_b, 0, 2, siu, PLAN_U, 3, 3)
-    near_sends(FINE_BACK, siu, riu, PLAN_U)
     for n, offset in enumerate(WIDE):
         to = WIDE_STARTS[n]
         for k in range(6):

time: 49.9 us -> 46.5 us (0.932)
  Pallas kernels: 48.2 us -> 44.8 us
    pallas_call x1, Pallas kernels: 48.2 us -> 44.8 us  [local(): return call(absorption, beta_x, beta_y, beta_z, source, initial)]
where the time goes in v5:
time: 46.5 us; the launch traced here: 46.3 us
  Pallas kernels  44.8 us (96%)
  local copies, waits for them, and re-layouts  1.57 us (3%)
    pallas_call x1, Pallas kernels, local(): return call(absorption, beta_x, beta_y, beta_z, source, initial)  44.8 us
    unnamed x1, local copies, waits for them, and re-layouts  1.57 us

profile of v5, /device:TPU:1, one launch (start us, length us, event | category | flops | bytes accessed | tf_op | source)
XLA Modules:
  0.0 46.3 jit_solution(16767064179701392858)
XLA Ops:
  0.0 44.8 %vcycle.1 = f32[8,16,256]{2,1,0:T(8,128)} custom-call(f32[8,16,256]{2,1,0:T(8,128)} %refs_0_.1, f32[8,16,256]{2,1,0:T(8,128)} %refs_1_.1, f32[8,16,256]{2,1,0:T(8,128)} %refs_2_.1, f32[8,16,256]{2,1,0:T(8,128)} %refs_3_.1, f32[8,16,256]{2,1,0:T(8,128)} %refs_4_.1, f32[8,16,256]{2,1,0:T(8,128)} %refs_5_.1), custom_call_target="tpu_custom_call" | custom-call | tf_op jit(solution)/shard_map/vcycle/pallas_call | solution.py:751
  44.8 1.6 %copy.8 = f32[8,16,256]{2,1,0:T(8,128)} copy(f32[8,16,256]{2,1,0:T(8,128)} %vcycle.1) | data formatting | bytes 262144

commit v6 on v5

--- a/solution.py
+++ b/solution.py
@@ -9,7 +9,7 @@
 COARSE_SWEEPS = 8
 LANES = 128
 HALF = 64
-GROUP = 8
+GROUP = 24
 MESH = pl.DeviceIdType.MESH
 
 NX0, NY0, HX0, HY0, YP0 = 8, 16, 5, 5, 26

time: 46.5 us -> 45.9 us (0.987)
  Pallas kernels: 44.8 us -> 44.2 us
    pallas_call x1, Pallas kernels: 44.8 us -> 44.2 us  [local(): return call(absorption, beta_x, beta_y, beta_z, source, initial)]
where the time goes in v6:
time: 45.9 us; the launch traced here: 45.7 us
  Pallas kernels  44.2 us (96%)
  local copies, waits for them, and re-layouts  1.57 us (3%)
    pallas_call x1, Pallas kernels, local(): return call(absorption, beta_x, beta_y, beta_z, source, initial)  44.2 us
    unnamed x1, local copies, waits for them, and re-layouts  1.57 us

profile of v6, /device:TPU:1, one launch (start us, length us, event | category | flops | bytes accessed | tf_op | source)
XLA Modules:
  0.0 45.7 jit_solution(17894666996227529187)
XLA Ops:
  0.0 44.2 %vcycle.1 = f32[8,16,256]{2,1,0:T(8,128)} custom-call(f32[8,16,256]{2,1,0:T(8,128)} %refs_0_.1, f32[8,16,256]{2,1,0:T(8,128)} %refs_1_.1, f32[8,16,256]{2,1,0:T(8,128)} %refs_2_.1, f32[8,16,256]{2,1,0:T(8,128)} %refs_3_.1, f32[8,16,256]{2,1,0:T(8,128)} %refs_4_.1, f32[8,16,256]{2,1,0:T(8,128)} %refs_5_.1), custom_call_target="tpu_custom_call" | custom-call | tf_op jit(solution)/shard_map/vcycle/pallas_call | solution.py:751
  44.2 1.6 %copy.8 = f32[8,16,256]{2,1,0:T(8,128)} copy(f32[8,16,256]{2,1,0:T(8,128)} %vcycle.1) | data formatting | bytes 262144
